TPU v7x, 512 devices: a whole 4x4x16 slice. The times are simulated.
512 devices in a mesh: obs: 8 (over y, core), cell: 64 (over x, z).
Axes of the slice: x: 4, y: 4, z: 16, core: 2. Of those that a mesh axis runs over, the one named last changes fastest.
Arguments:
- station_xy: float32 [2, 32768], P(None, 'obs'), may hold values from 0 to 8
- station_alt: float32 [32768], P('obs'), may hold values from 0.02 to 0.06
- cell_xy: float32 [2, 262144], P(None, 'cell'), may hold values from 0 to 8
- cell_depth: float32 [262144], P('cell'), may hold values from 0.04 to 0.12
- members: float32 [262144, 128], P('cell', 'obs'), may hold values from -6 to 6
- targets: float32 [32768, 128], P('obs'), may hold values from -9 to 9
- noise_var: float32 [32768], P('obs'), may hold values from 0.1 to 10
Outputs:
- increment: float32 [262144, 128], P('cell', 'obs')
All inputs are finite; a program needn't handle non-finite values.
Results may differ from a plain program's by a relative error of at most 0.0006.
Values sent between devices are 32-bit elements; how exact they have to be, the bound alone decides.
A program may use at most 64 MiB of HBM per device.

v0:
```python
import math

import jax
import jax.numpy as jnp
from jax import lax
from jax.sharding import PartitionSpec as P


def kernel_rows(pos_x, pos_y, height, cell_xy, cell_depth, strength):
    delta_x = pos_x[:, None] - cell_xy[0][None, :]
    delta_y = pos_y[:, None] - cell_xy[1][None, :]
    depth_sum = height[:, None] + cell_depth[None, :]
    radius_sq = delta_x * delta_x + delta_y * delta_y + depth_sum * depth_sum
    inverse = lax.rsqrt(radius_sq)
    return (strength * depth_sum * inverse * inverse * inverse).astype(jnp.bfloat16)


def moments(predicted, targets, noise_var):
    pred_anom = predicted - jnp.mean(predicted, axis=1, keepdims=True)
    innovation = targets - predicted
    weighted = pred_anom / noise_var[:, None]
    gram_part = jnp.dot(weighted.T, pred_anom, precision=lax.Precision.HIGHEST)
    cross_part = jnp.dot(weighted.T, innovation, precision=lax.Precision.HIGHEST)
    return (gram_part, cross_part)


def per_device(station_xy, station_alt, cell_xy, cell_depth, members, targets, noise_var):
    all_members = lax.all_gather(members, "obs", axis=1, tiled=True)
    width = all_members.shape[1]
    total_cells = cell_xy.shape[1] * lax.axis_size("cell")
    strength = 1.0 / math.sqrt(total_cells)
    member_low = all_members.astype(jnp.bfloat16)
    station_rows = station_alt.shape[0]
    block_rows = math.gcd(256, station_rows)
    block_count = station_rows // block_rows
    pos_x = station_xy[0].reshape(block_count, block_rows)
    pos_y = station_xy[1].reshape(block_count, block_rows)
    height = station_alt.reshape(block_count, block_rows)

    def one_block(inputs):
        kernel = kernel_rows(inputs[0], inputs[1], inputs[2], cell_xy, cell_depth, strength)
        return jnp.dot(kernel, member_low, preferred_element_type=jnp.float32)

    partial_pred = lax.map(one_block, (pos_x, pos_y, height)).reshape(station_rows, width)
    predicted = lax.psum(partial_pred, "cell")
    gram_part, cross_part = moments(predicted, targets, noise_var)
    gram_sum, cross = lax.psum((gram_part, cross_part), "obs")
    gram_matrix = gram_sum + (width - 1.0) * jnp.eye(width, dtype=jnp.float32)
    factor = jnp.linalg.cholesky(gram_matrix)
    interim = lax.linalg.triangular_solve(factor, cross, left_side=True, lower=True)
    coeffs = lax.linalg.triangular_solve(
        factor, interim, left_side=True, lower=True, transpose_a=True
    )
    own_members = members.shape[1]
    own_coeffs = lax.dynamic_slice_in_dim(
        coeffs, lax.axis_index("obs") * own_members, own_members, 1
    )
    member_anom = all_members - jnp.mean(all_members, axis=1, keepdims=True)
    return jnp.dot(member_anom, own_coeffs, precision=lax.Precision.HIGHEST)


def solution(mesh):
    placed = (
        P(None, "obs"),
        P("obs"),
        P(None, "cell"),
        P("cell"),
        P("cell", "obs"),
        P("obs", None),
        P("obs"),
    )
    return jax.shard_map(
        per_device, mesh=mesh, in_specs=placed, out_specs=P("cell", "obs"), check_vma=False
    )
```

profile of v0, /device:TPU:1, one launch (start us, length us, event | category | flops | bytes accessed | tf_op | source)
XLA Modules:
  0.0 492.4 jit_solution(16282921532002146175)
XLA Ops:
  7.3 0.9 slice_reduce_fusion
  8.3 0.7 reshape.33
  9.0 39.1 %all-gather.2.cloned.1.call-done = f32[4096,128]{0,1:T(8,128)} async-done(((f32[4096,16]{0,1:T(8,128)}), f32[4096,128]{0,1:T(8,128)}) %all-gather.2.cloned.1.call-update) | async-done | bytes 2097168 | tf_op jit(solution)/shard_map/all_gather | solution.py:28
  48.1 2.4 fusion.32
  51.3 45.5 %while.10 = (s32[]{:T(128)}, f32[16,256,128]{2,1,0:T(8,128)}, f32[16,256]{1,0:T(8,128)S(1)}, f32[4096]{0:T(1024)S(1)}, f32[16,256]{1,0:T(8,128)S(1)}, /*index=5*...) while((s32[]{:T(128)}, f32[16,256,128]{2,1,0:T(8,128)}, ...), condition=%wide.region_2.3_spmd, body=%wide.region_1.2_spmd.sunk | while | flops 282066944 | bytes 1304165 | solution.py:44
  51.3 2.8 fusion.43
  54.2 2.8 fusion.43
  57.0 2.8 fusion.43
  59.9 2.8 fusion.43
  62.7 2.8 fusion.43
  65.5 2.8 fusion.43
  68.4 2.8 fusion.43
  71.2 2.8 fusion.43
  74.1 2.8 fusion.43
  76.9 2.8 fusion.43
  79.8 2.8 fusion.43
  82.6 2.8 fusion.43
  85.5 2.8 fusion.43
  88.3 2.8 fusion.43
  91.2 2.8 fusion.43
  94.0 2.8 fusion.43
  97.1 268.8 %all-reduce.4.cloned.1.call-done = f32[4096,128]{1,0:T(8,128)} async-done(((f32[4096,128]{1,0:T(8,128)}), f32[4096,128]{1,0:T(8,128)}) %all-reduce.4.cloned.1.call-update) | async-done | bytes 2097168 | tf_op jit(solution)/shard_map/psum | solution.py:45
  365.8 2.4 reduce_sum.19
  368.2 5.9 %fusion.16 = f32[128,128]{1,0:T(8,128)} fusion(f32[4096,128]{1,0:T(8,128)S(1)} %copy-done.1, f32[4096]{0:T(1024)S(1)} %copy-done.6, f32[4096]{0:T(1024)S(1)} %broadcast_multiply_fusion), kind=kOutput, calls=%fused_computation.17 | convolution fusion | flops 806879232 | bytes 2195456 | tf_op jit(solution)/shard_map/dot_general | solution.py:22
  374.1 5.5 %fusion.12 = f32[128,128]{1,0:T(8,128)} fusion(f32[4096,128]{1,0:T(8,128)S(1)} %copy-done.4, f32[4096,128]{1,0:T(8,128)S(1)} %copy-done.2, f32[4096]{0:T(1024)S(1)} %copy-done.6, f32[4096]{0:T(1024)S(1)} %broadcast_multiply_fusion), kind=kOutput, calls=%fused_computation.13 | convolution fusion | flops 806879232 | bytes 4292608 | tf_op jit(solution)/shard_map/dot_general | solution.py:23
  379.7 77.9 %all-reduce.6.cloned.1.call-done = (f32[128,128]{1,0:T(8,128)}, f32[128,128]{1,0:T(8,128)}) async-done(((f32[128,128]{1,0:T(8,128)}, f32[128,128]{1,0:T(8,128)}), (f32[128,128]{1,0:T(8,128)}, f32[128,128]{1,0:T(8,128)})) %all-reduce.6.cloned.1.call-update) | async-done | bytes 131088 | tf_op jit(solution)/shard_map/psum | solution.py:47
  457.6 0.9 select_add_fusion
  458.5 0.9 fusion.28
  459.4 11.9 %cholesky.16 = f32[128,128]{1,0:T(8,128)S(1)} custom-call(f32[128,128]{1,0:T(8,128)S(1)} %fusion.28), custom_call_target="Cholesky" | custom-call | tf_op jit(solution)/shard_map/jit(cholesky)/cholesky | solution.py:49
  472.7 9.8 %custom-call.8 = f32[1,128,128]{1,2,0:T(8,128)S(1)} custom-call(f32[1,128,128]{2,1,0:T(8,128)S(1)} %fusion.23), custom_call_target="InvertDiagBlocksLowerTriangular" | custom-call | tf_op jit(solution)/shard_map/triangular_solve | solution.py:51
  482.5 1.1 fusion.26
  483.8 2.0 fusion.14
  (79 shorter events, 4.0 us)
Async XLA Ops:
  6.5 41.6 %all-gather.2.cloned.1.call-start = ((), (), s32[]{:S(2)}) async-start(), calls=%async_computation | async-start | bytes 2359296 | tf_op jit(solution)/shard_map/all_gather | solution.py:28
  7.3 358.6 %all-reduce.4.cloned.1.call-start = ((), (), s32[]{:S(2)}) async-start(), calls=%async_computation.1 | async-start | bytes 4194304 | tf_op jit(solution)/shard_map/psum | solution.py:45
  9.0 42.3 %copy-start.3 = (f32[2,4096]{1,0:T(2,128)S(1)}, f32[2,4096]{1,0:T(2,128)}, u32[]{:S(2)}) copy-start(f32[2,4096]{1,0:T(2,128)} %param.11) | copy-start | bytes 98308
  9.0 42.3 %copy-start.5 = (f32[4096]{0:T(1024)S(1)}, f32[4096]{0:T(1024)}, u32[]{:S(2)}) copy-start(f32[4096]{0:T(1024)} %param.12) | copy-start | bytes 49156
  96.8 271.4 %copy-start.6 = (f32[4096]{0:T(1024)S(1)}, f32[4096]{0:T(1024)}, u32[]{:S(2)}) copy-start(f32[4096]{0:T(1024)} %param.15) | copy-start | bytes 49156
  96.8 360.8 %all-reduce.6.cloned.1.call-start = ((), (), s32[]{:S(2)}) async-start(), calls=%async_computation.2 | async-start | bytes 262144 | tf_op jit(solution)/shard_map/psum | solution.py:47
  365.8 2.4 copy-start.1
  368.2 5.9 %copy-start.2 = (f32[4096,128]{1,0:T(8,128)S(1)}, f32[4096,128]{1,0:T(8,128)}, u32[]{:S(2)}) copy-start(f32[4096,128]{1,0:T(8,128)} %all-reduce.4.cloned.1.call-done) | copy-start | bytes 6291460
  368.2 5.9 %copy-start.4 = (f32[4096,128]{1,0:T(8,128)S(1)}, f32[4096,128]{1,0:T(8,128)}, u32[]{:S(2)}) copy-start(f32[4096,128]{1,0:T(8,128)} %param.14) | copy-start | bytes 6291460
  374.1 109.7 %copy-start = (f32[4096,128]{0,1:T(8,128)S(1)}, f32[4096,128]{0,1:T(8,128)}, u32[]{:S(2)}) copy-start(f32[4096,128]{0,1:T(8,128)} %all-gather.2.cloned.1.call-done) | copy-start | bytes 6291460
Sparse Core Ops, SparseCore 0:
  9.5 38.5 all-gather.1
  96.9 268.8 all-reduce.3
  379.8 77.7 all-reduce.5
where the time goes:
time: 493 us; the launch traced here: 492 us
  waiting for transfers between devices  387 us (78%)
  matrix products  59.4 us (12%)
  other arithmetic  29.6 us (6%)
  between operations  13.3 us (3%)
    psum x1, waiting for transfers between devices, per_device(): predicted = lax.psum(partial_pred, 'cell')  269 us
    psum x1, waiting for transfers between devices, per_device(): gram_sum, cross = lax.psum((gram_part, cross_part), 'obs')  77.9 us
    dot_general x16, matrix products, one_block(): return jnp.dot(kernel, member_low, preferred_element_type=jnp.float32)  44.7 us
    all_gather x1, waiting for transfers between devices, per_device(): all_members = lax.all_gather(members, 'obs', axis=1, tiled=True)  39.1 us
    another operation x3, other arithmetic, per_device(): factor = jnp.linalg.cholesky(gram_matrix)  12.6 us
    another operation x2, other arithmetic, per_device(): lax.linalg.triangular_solve(factor, interim, left_side=True, lower=True,...  10.5 us
  transfers between devices with their start and end apart: 3, of which 3 were waited for; matrix products, arithmetic and copies ran while one was open for 0% of the time, Pallas kernels for 0%

commit v1 on v0

v1 whole, which is shorter than its diff:
```python
import functools
import math

import jax
import jax.numpy as jnp
from jax import lax
from jax.experimental import pallas as pl
from jax.experimental.pallas import tpu as pltpu
from jax.sharding import PartitionSpec as P

MESH = pl.DeviceIdType.MESH
LANES = 128
WIDE = 512


def dot32(a, b, dims):
    return lax.dot_general(
        a, b, (dims, ((), ())), precision=lax.Precision.HIGHEST, preferred_element_type=jnp.float32
    )


def sums_kernel(nx, ny, nz, xy, alt, cell_xy, cell_dep, own, targets, noise,
                gathered_out, gram_out, cross_out,
                full, low, part, ring_in, x_in, tgt, wide_noise, rows, quarter, obs_in, eighth, z_in, group, total,
                g_send, g_recv, r_send, r_recv, x_send, x_recv, a_send, a_recv, o_send, o_recv,
                z_send, z_recv, b_send, b_recv, c_send, c_recv, local):
    obs, cell = lax.axis_index("obs"), lax.axis_index("cell")
    y, core = obs // 2, lax.rem(obs, 2)
    x, z = cell // nz, lax.rem(cell, nz)
    no = 2 * ny
    mine, cells = own.shape
    width = full.shape[0]
    stations = part.shape[0]
    chunk = stations // nz
    half = chunk // 2
    final = chunk // nx

    def obs_of(yy, cc):
        return lax.rem(yy + 2 * ny, ny) * 2 + cc

    def cell_of(xx, zz):
        return lax.rem(xx + 2 * nx, nx) * nz + lax.rem(zz + 4 * nz, nz)

    barrier = pltpu.get_barrier_semaphore()
    peers = [{"obs": lax.rem(obs + o, no)} for o in range(1, no)]
    peers += [{"cell": cell_of(x + o, z)} for o in range(1, nx)]
    peers += [{"cell": cell_of(x, z + o)} for o in range(1, nz)]
    for peer in peers:
        pl.semaphore_signal(barrier, inc=1, device_id=peer, device_id_type=MESH)

    mine_rows = pl.ds(pl.multiple_of(obs * mine, mine), mine)
    get_own = pltpu.make_async_copy(own, full.at[mine_rows], local.at[0])
    get_own.start()
    first = pl.multiple_of(z * chunk + x * final, final)
    get_tgt = pltpu.make_async_copy(targets.at[pl.ds(first, final)], tgt, local.at[1])
    get_tgt.start()
    get_own.wait()
    pl.semaphore_wait(barrier, len(peers))

    cut = cells // 2
    left, right, whole = pl.ds(0, cut), pl.ds(cut, cut), pl.ds(0, cells)

    def push(block, cols, target, slot):
        at = pl.ds(pl.multiple_of(block * mine, mine), mine)
        return pltpu.make_async_remote_copy(
            src_ref=full.at[at, cols], dst_ref=full.at[at, cols],
            send_sem=g_send.at[slot], recv_sem=g_recv.at[slot],
            device_id={"obs": target}, device_id_type=MESH,
        )

    mate, up, down = obs_of(y, 1 - core), obs_of(y + 1, core), obs_of(y - 1, core)
    far = obs_of(y + 2, core)
    sends = [push(obs, whole, mate, 0), push(obs, whole, up, 1), push(obs, whole, down, 2)]
    for c in sends:
        c.start()
    push(down, whole, up, 1).wait_recv()
    more = [push(down, left, up, 3), push(down, whole, mate, 4)]
    for c in more:
        c.start()
    sends += more
    push(up, whole, down, 2).wait_recv()
    more = [push(up, right, down, 5), push(up, whole, mate, 6)]
    for c in more:
        c.start()
    sends += more
    push(far, left, up, 3).wait_recv()
    more = [push(far, left, mate, 7)]
    more[0].start()
    sends += more
    push(far, right, down, 5).wait_recv()
    more = [push(far, right, mate, 8)]
    more[0].start()
    sends += more
    for slot, block, cols in (
        (0, mate, whole), (4, obs_of(y - 1, 1 - core), whole), (6, obs_of(y + 1, 1 - core), whole),
        (7, obs_of(y + 2, 1 - core), left), (8, obs_of(y + 2, 1 - core), right),
    ):
        push(block, cols, mate, slot).wait_recv()
    for c in sends:
        c.wait_send()
    save = pltpu.make_async_copy(full, gathered_out, local.at[2])
    save.start()
    for j in range(0, cells, WIDE):
        low[:, j:j + WIDE] = full[:, j:j + WIDE].astype(jnp.bfloat16)

    def ring_rows(way, step):
        at = lax.rem(z - 1 - step + 2 * nz, nz) if way == 0 else lax.rem(z + 1 + step, nz)
        return pl.ds(pl.multiple_of(at * chunk + way * half, half), half)

    def ring_copy(way, step):
        return pltpu.make_async_remote_copy(
            src_ref=part.at[ring_rows(way, step)], dst_ref=ring_in.at[way, step],
            send_sem=r_send.at[way, step], recv_sem=r_recv.at[way, step],
            device_id={"cell": cell_of(x, z + 1 - 2 * way)}, device_id_type=MESH,
        )

    def column(ref, row, at):
        tile = jnp.broadcast_to(ref[row:row + 1, at], (half, half)).T
        return jnp.concatenate([tile] * (WIDE // LANES), axis=1)

    def compute(step):
        ats = [ring_rows(0, step), ring_rows(1, step)]
        pos_x = jnp.concatenate([column(xy, 0, at) for at in ats], axis=0)
        pos_y = jnp.concatenate([column(xy, 1, at) for at in ats], axis=0)
        height = jnp.concatenate([column(alt, 0, at) for at in ats], axis=0)
        acc = jnp.zeros((chunk, width), jnp.float32)
        for j in range(0, cells, WIDE):
            dx = pos_x - cell_xy[0:1, j:j + WIDE]
            dy = pos_y - cell_xy[1:2, j:j + WIDE]
            h = height + cell_dep[0:1, j:j + WIDE]
            inverse = lax.rsqrt(dx * dx + dy * dy + h * h)
            kernel = ((h * inverse) * (inverse * inverse)).astype(jnp.bfloat16)
            acc += lax.dot_general(
                kernel, low[:, j:j + WIDE], (((1,), (1,)), ((), ())), preferred_element_type=jnp.float32
            )
        part[ats[0], :] = acc[:half]
        part[ats[1], :] = acc[half:]

    def ring_step(step, carry):
        compute(step)

        @pl.when(step > 0)
        def _():
            for way in range(2):
                ring_copy(way, step - 1).wait_recv()
                at = ring_rows(way, step)
                part[at, :] = part[at, :] + ring_in[way, step - 1]

        @pl.when(step < nz - 1)
        def _():
            for way in range(2):
                ring_copy(way, step).start()

        return carry

    lax.fori_loop(0, nz, ring_step, 0)

    x_copies = []
    for o in range(1, nx):
        to = lax.rem(x + o, nx)
        x_copies.append(pltpu.make_async_remote_copy(
            src_ref=part.at[pl.ds(pl.multiple_of(z * chunk + to * final, final), final)],
            dst_ref=x_in.at[o - 1], send_sem=x_send.at[o - 1], recv_sem=x_recv.at[o - 1],
            device_id={"cell": cell_of(x + o, z)}, device_id_type=MESH,
        ))
        x_copies[-1].start()
    window = pl.ds(pl.multiple_of(z * chunk + (x // 2) * LANES, LANES), LANES)
    wide_noise[...] = jnp.broadcast_to(noise[0:1, window], (LANES, LANES)).T
    variance = wide_noise[pl.ds(pl.multiple_of(lax.rem(x, 2) * final, final), final), :]
    get_tgt.wait()
    for c in x_copies:
        c.wait_recv()
    predicted = part[pl.ds(first, final), :]
    for o in range(nx - 1):
        predicted = predicted + x_in[o]
    predicted = predicted * (1.0 / math.sqrt(cells * nx * nz))

    anomaly = predicted - jnp.mean(predicted, axis=1, keepdims=True)
    weighted = anomaly / variance
    rows[0:width, :] = dot32(anomaly, weighted, ((0,), (0,)))
    rows[width:, :] = dot32(tgt[...] - predicted, weighted, ((0,), (0,)))

    deep = rows.shape[0] // nx
    thin = deep // no
    copies = []
    for o in range(1, nx):
        to = lax.rem(x + o, nx)
        copies.append(pltpu.make_async_remote_copy(
            src_ref=rows.at[pl.ds(pl.multiple_of(to * deep, deep), deep)],
            dst_ref=quarter.at[o - 1], send_sem=a_send.at[o - 1], recv_sem=a_recv.at[o - 1],
            device_id={"cell": cell_of(x + o, z)}, device_id_type=MESH,
        ))
        copies[-1].start()
    for c in copies:
        c.wait_recv()
    my_deep = pl.ds(pl.multiple_of(x * deep, deep), deep)
    value = rows[my_deep, :]
    for o in range(nx - 1):
        value = value + quarter[o]
    group[...] = value
    stage = []
    for o in range(1, no):
        to = lax.rem(obs + o, no)
        stage.append(pltpu.make_async_remote_copy(
            src_ref=group.at[pl.ds(pl.multiple_of(to * thin, thin), thin)],
            dst_ref=obs_in.at[o - 1], send_sem=o_send.at[o - 1], recv_sem=o_recv.at[o - 1],
            device_id={"obs": to}, device_id_type=MESH,
        ))
        stage[-1].start()
    for c in stage:
        c.wait_recv()
    copies += stage
    my_thin = pl.ds(pl.multiple_of(obs * thin, thin), thin)
    value = group[my_thin, :]
    for o in range(no - 1):
        value = value + obs_in[o]
    eighth[...] = value
    stage = []
    for o in range(1, nz):
        stage.append(pltpu.make_async_remote_copy(
            src_ref=eighth, dst_ref=z_in.at[o - 1], send_sem=z_send.at[o - 1], recv_sem=z_recv.at[o - 1],
            device_id={"cell": cell_of(x, z + o)}, device_id_type=MESH,
        ))
        stage[-1].start()
    for c in stage:
        c.wait_recv()
    copies += stage
    for o in range(nz - 1):
        value = value + z_in[o]
    back = pl.ds(pl.multiple_of(x * deep + obs * thin, thin), thin)
    total[back, :] = value
    stage = []
    for o in range(1, no):
        stage.append(pltpu.make_async_remote_copy(
            src_ref=total.at[back], dst_ref=total.at[back], send_sem=b_send.at[o - 1], recv_sem=b_recv.at[o - 1],
            device_id={"obs": lax.rem(obs + o, no)}, device_id_type=MESH,
        ))
        stage[-1].start()
    for o in range(1, no):
        at = pl.ds(pl.multiple_of(x * deep + lax.rem(obs + no - o, no) * thin, thin), thin)
        pltpu.make_async_remote_copy(
            src_ref=total.at[at], dst_ref=total.at[at], send_sem=b_send.at[o - 1], recv_sem=b_recv.at[o - 1],
            device_id={"obs": lax.rem(obs + o, no)}, device_id_type=MESH,
        ).wait_recv()
    copies += stage
    stage = []
    for o in range(1, nx):
        stage.append(pltpu.make_async_remote_copy(
            src_ref=total.at[my_deep], dst_ref=total.at[my_deep], send_sem=c_send.at[o - 1],
            recv_sem=c_recv.at[o - 1], device_id={"cell": cell_of(x + o, z)}, device_id_type=MESH,
        ))
        stage[-1].start()
    for o in range(1, nx):
        at = pl.ds(pl.multiple_of(lax.rem(x + nx - o, nx) * deep, deep), deep)
        pltpu.make_async_remote_copy(
            src_ref=total.at[at], dst_ref=total.at[at], send_sem=c_send.at[o - 1],
            recv_sem=c_recv.at[o - 1], device_id={"cell": cell_of(x + o, z)}, device_id_type=MESH,
        ).wait_recv()
    copies += stage
    gram_out[...] = total[0:width, :]
    cross_out[...] = total[pl.ds(pl.multiple_of(width + obs * mine, mine), mine), :]

    for c in x_copies + copies:
        c.wait_send()

    def drain(step, carry):
        for way in range(2):
            ring_copy(way, step).wait_send()
        return carry

    lax.fori_loop(0, nz - 1, drain, 0)
    save.wait()


def per_device(nx, ny, nz, station_xy, station_alt, cell_xy, cell_depth, members, targets, noise_var):
    own = members.T
    mine, cells = own.shape
    no = 2 * ny
    width = mine * no
    stations = station_alt.shape[0]
    chunk = stations // nz
    half, final = chunk // 2, chunk // nx
    deep = 2 * width // nx
    thin = deep // no
    f32 = jnp.float32
    vmem = pl.BlockSpec(memory_space=pltpu.VMEM)
    anyw = pl.BlockSpec(memory_space=pl.ANY)
    dma = pltpu.SemaphoreType.DMA
    gathered, gram, cross = pl.pallas_call(
        functools.partial(sums_kernel, nx, ny, nz),
        out_shape=(
            jax.ShapeDtypeStruct((width, cells), f32),
            jax.ShapeDtypeStruct((width, width), f32),
            jax.ShapeDtypeStruct((mine, width), f32),
        ),
        in_specs=[vmem, vmem, vmem, vmem, anyw, anyw, vmem],
        out_specs=(anyw, vmem, vmem),
        scratch_shapes=[
            pltpu.VMEM((width, cells), f32),
            pltpu.VMEM((width, cells), jnp.bfloat16),
            pltpu.VMEM((stations, width), f32),
            pltpu.VMEM((2, nz - 1, half, width), f32),
            pltpu.VMEM((nx - 1, final, width), f32),
            pltpu.VMEM((final, width), f32),
            pltpu.VMEM((LANES, LANES), f32),
            pltpu.VMEM((2 * width, width), f32),
            pltpu.VMEM((nx - 1, deep, width), f32),
            pltpu.VMEM((no - 1, thin, width), f32),
            pltpu.VMEM((thin, width), f32),
            pltpu.VMEM((nz - 1, thin, width), f32),
            pltpu.VMEM((deep, width), f32),
            pltpu.VMEM((2 * width, width), f32),
            dma((9,)), dma((9,)),
            dma((2, nz - 1)), dma((2, nz - 1)),
            dma((nx - 1,)), dma((nx - 1,)),
            dma((nx - 1,)), dma((nx - 1,)),
            dma((no - 1,)), dma((no - 1,)),
            dma((nz - 1,)), dma((nz - 1,)),
            dma((no - 1,)), dma((no - 1,)),
            dma((nx - 1,)), dma((nx - 1,)),
            dma((3,)),
        ],
        compiler_params=pltpu.CompilerParams(
            collective_id=0, has_side_effects=True, vmem_limit_bytes=48 * 2**20
        ),
    )(station_xy, station_alt[None], cell_xy, cell_depth[None], own, targets, noise_var[None])
    matrix = gram + (width - 1.0) * jnp.eye(width, dtype=f32)
    factor = jnp.linalg.cholesky(matrix)
    interim = lax.linalg.triangular_solve(factor, cross.T, left_side=True, lower=True)
    coeffs = lax.linalg.triangular_solve(factor, interim, left_side=True, lower=True, transpose_a=True)
    coeffs = coeffs - jnp.mean(coeffs, axis=0, keepdims=True)
    return jnp.dot(gathered.T, coeffs, precision=lax.Precision.HIGHEST)


def solution(mesh):
    nz = 16
    nx = mesh.shape["cell"] // nz
    ny = mesh.shape["obs"] // 2
    placed = (
        P(None, "obs"),
        P("obs"),
        P(None, "cell"),
        P("cell"),
        P("cell", "obs"),
        P("obs", None),
        P("obs"),
    )
    return jax.shard_map(
        functools.partial(per_device, nx, ny, nz),
        mesh=mesh, in_specs=placed, out_specs=P("cell", "obs"), check_vma=False,
    )
```

time: 493 us -> 154 us (0.31)
  waiting for transfers between devices: 387 us -> 0 us
  Pallas kernels: 0 us -> 121 us
  matrix products: 59.4 us -> 2.55 us
  between operations: 13.3 us -> 0.08 us
  other arithmetic: 29.6 us -> 22.9 us
    psum x2 -> x0, waiting for transfers between devices: 347 us -> none  [the longest x1 269 us: per_device(): predicted = lax.psum(partial_pred, 'cell')]
    pallas_call x0 -> x1, Pallas kernels: none -> 121 us  [per_device(): pl.pallas_call(functools.partial(sums_kernel, nx, ny, nz), out_shape=(jax...]
    dot_general x19 -> x1, matrix products: 58.1 us -> 1.91 us  [per_device(): return jnp.dot(gathered.T, coeffs, precision=lax.Precision.HIGHEST)]
    all_gather x1 -> x0, waiting for transfers between devices: 39.1 us -> none  [per_device(): all_members = lax.all_gather(members, 'obs', axis=1, tiled=True)]
    unnamed x14, local copies, waits for them, and re-layouts: 0.03 us -> 6.21 us
  transfers between devices with their start and end apart: 3 -> 0, of which waited for: 3 -> 0; matrix products, arithmetic and copies ran while one was open for 0% -> 0% of each run, Pallas kernels for 0% -> 0%
where the time goes in v1:
time: 154 us; the launch traced here: 153 us
  Pallas kernels  121 us (79%)
  other arithmetic  22.9 us (15%)
  local copies, waits for them, and re-layouts  6.29 us (4%)
  matrix products  2.55 us (2%)
    pallas_call x1, Pallas kernels, per_device(): pl.pallas_call(functools.partial(sums_kernel, nx, ny, nz), out_shape=(jax...  121 us
    another operation x3, other arithmetic, per_device(): factor = jnp.linalg.cholesky(matrix)  12.4 us
    another operation x2, other arithmetic, per_device(): lax.linalg.triangular_solve(factor, interim, left_side=True, lower=True,...  10.5 us
    unnamed x14, local copies, waits for them, and re-layouts  6.21 us

profile of v1, /device:TPU:1, one launch (start us, length us, event | category | flops | bytes accessed | tf_op | source)
XLA Modules:
  0.0 153.2 jit_solution(18247393562391598087)
XLA Ops:
  0.0 0.0 copy-start
  0.0 1.6 %copy-done = f32[4096,128]{1,0:T(8,128)S(1)} copy-done((f32[4096,128]{1,0:T(8,128)S(1)}, f32[4096,128]{1,0:T(8,128)}, u32[]{:S(2)}) %copy-start) | copy-done | bytes 2097176
  1.6 0.0 copy-start.1
  1.6 0.9 copy-done.1
  2.5 0.0 copy-start.2
  2.5 0.8 copy-done.2
  3.3 0.0 copy-start.3
  3.3 0.8 copy-done.3
  4.1 0.0 copy-start.4
  4.1 0.7 copy-done.4
  4.8 0.0 copy-start.5
  4.8 0.7 copy-done.5
  5.5 0.0 copy-start.6
  5.5 0.7 copy-done.6
  6.2 121.4 %shard_map.73 = (f32[128,4096]{1,0:T(8,128)S(1)}, f32[128,128]{1,0:T(8,128)S(1)}, f32[16,128]{1,0:T(8,128)S(1)}) custom-call(f32[2,4096]{1,0:T(2,128)S(1)} %copy-done.2, f32[1,4096]{1,0:T(1,128)S(1)} %bitcast.21, f32[2,4096]{1,0:T(2,128)S(1)} %copy-done.3, f32[1,4096]{1,0:T(1,128)S(1)} %bitcast.22, f32[16,4096]{1,0:T(8,128)S(1)} %bitcast.20, ...), custom_call_target="tpu_custom_call" | custom-call | tf_op jit(solution)/shard_map/pallas_call | solution.py:289
  127.6 0.1 copy.8
  127.7 11.7 %cholesky.16 = f32[128,128]{1,0:T(8,128)S(1)} custom-call(f32[128,128]{1,0:T(8,128)S(1)} %fusion.5), custom_call_target="Cholesky" | custom-call | tf_op jit(solution)/shard_map/jit(cholesky)/cholesky | solution.py:328
  139.5 0.6 compare_reduce_fusion
  140.1 0.7 fusion
  140.8 9.8 %custom-call.8 = f32[1,128,128]{1,2,0:T(8,128)S(1)} custom-call(f32[1,128,128]{2,1,0:T(8,128)S(1)} %fusion), custom_call_target="InvertDiagBlocksLowerTriangular" | custom-call | tf_op jit(solution)/shard_map/triangular_solve | solution.py:330
  150.6 0.3 fusion.3
  150.9 0.4 fusion.9
  151.3 1.9 %fusion.6 = f32[4096,16]{0,1:T(8,128)} fusion(f32[128,4096]{1,0:T(8,128)S(1)} %get-tuple-element.8, f32[128,16]{0,1:T(8,128)S(1)} %get-tuple-element.12, f32[16]{0:T(128)S(1)} %broadcast_multiply_fusion), kind=kOutput, calls=%fused_computation.12 | convolution fusion | flops 100665344 | bytes 2367552 | tf_op jit(solution)/shard_map/dot_general | solution.py:332
  (4 shorter events, 0.1 us)
Async XLA Ops:
  0.0 1.6 %copy-start = (f32[4096,128]{1,0:T(8,128)S(1)}, f32[4096,128]{1,0:T(8,128)}, u32[]{:S(2)}) copy-start(f32[4096,128]{1,0:T(8,128)} %targets.1) | copy-start | bytes 6291460
  1.6 0.9 copy-start.1
  2.5 0.8 copy-start.2
  3.3 0.8 copy-start.3
  4.1 0.7 copy-start.4
  4.8 0.7 copy-start.5
  5.5 0.7 copy-start.6

commit v2 on v1

v2 whole, which is shorter than its diff:
```python
import functools
import math

import jax
import jax.numpy as jnp
from jax import lax
from jax.experimental import pallas as pl
from jax.experimental.pallas import tpu as pltpu
from jax.sharding import PartitionSpec as P

MESH = pl.DeviceIdType.MESH
SUB = 8
LANES = 128
WIDE = 512


def dot32(a, b, dims):
    return lax.dot_general(
        a, b, (dims, ((), ())), precision=lax.Precision.HIGHEST, preferred_element_type=jnp.float32
    )


def sums_kernel(nx, ny, nz, xy_in, alt_in, cell_xy_in, cell_dep_in, own, targets, noise_in,
                gathered_out, gram_out, cross_out,
                xy, alt, cell_xy, cell_dep, noise,
                full, low, part, ring_in, x_in, tgt, wide_noise, rows, plane_in, eighth, z_in, total,
                g_send, g_recv, r_send, r_recv, x_send, x_recv, a_send, a_recv,
                z_send, z_recv, b_send, b_recv, local):
    obs, cell = lax.axis_index("obs"), lax.axis_index("cell")
    y, core = obs // 2, lax.rem(obs, 2)
    x, z = cell // nz, lax.rem(cell, nz)
    no = 2 * ny
    mine, cells = own.shape
    width = full.shape[0]
    stations = part.shape[0]
    chunk = stations // nz
    half = chunk // 2
    final = chunk // nx

    def obs_of(yy, cc):
        return lax.rem(yy + 2 * ny, ny) * 2 + cc

    def cell_of(xx, zz):
        return lax.rem(xx + 2 * nx, nx) * nz + lax.rem(zz + 4 * nz, nz)

    barrier = pltpu.get_barrier_semaphore()
    peers = [{"obs": o} for o in (obs_of(y, 1 - core), obs_of(y + 1, core), obs_of(y - 1, core))]
    peers += [{"cell": cell_of(x, z + 1)}, {"cell": cell_of(x, z - 1)}]
    peers += [{"cell": cell_of(x + o, z)} for o in range(1, nx)]
    for peer in peers:
        pl.semaphore_signal(barrier, inc=1, device_id=peer, device_id_type=MESH)

    mine_rows = pl.ds(pl.multiple_of(obs * mine, mine), mine)
    first = pl.multiple_of(z * chunk + x * final, final)
    loads = [
        pltpu.make_async_copy(src, dst, local.at[i]) for i, (src, dst) in enumerate((
            (own, full.at[mine_rows]), (xy_in, xy), (alt_in, alt), (cell_xy_in, cell_xy),
            (cell_dep_in, cell_dep), (noise_in, noise), (targets.at[pl.ds(first, final)], tgt),
        ))
    ]
    for c in loads:
        c.start()
    loads[0].wait()
    pl.semaphore_wait(barrier, len(peers))

    cut = cells // 2
    left, right, whole = pl.ds(0, cut), pl.ds(cut, cut), pl.ds(0, cells)

    def push(block, cols, target, slot):
        at = pl.ds(pl.multiple_of(block * mine, mine), mine)
        return pltpu.make_async_remote_copy(
            src_ref=full.at[at, cols], dst_ref=full.at[at, cols],
            send_sem=g_send.at[slot], recv_sem=g_recv.at[slot],
            device_id={"obs": target}, device_id_type=MESH,
        )

    mate, up, down = obs_of(y, 1 - core), obs_of(y + 1, core), obs_of(y - 1, core)
    far = obs_of(y + 2, core)
    sends = [push(obs, whole, mate, 0), push(obs, whole, up, 1), push(obs, whole, down, 2)]
    for c in sends:
        c.start()
    push(down, whole, up, 1).wait_recv()
    more = [push(down, left, up, 3), push(down, whole, mate, 4)]
    for c in more:
        c.start()
    sends += more
    push(up, whole, down, 2).wait_recv()
    more = [push(up, right, down, 5), push(up, whole, mate, 6)]
    for c in more:
        c.start()
    sends += more
    push(far, left, up, 3).wait_recv()
    more = [push(far, left, mate, 7)]
    more[0].start()
    sends += more
    push(far, right, down, 5).wait_recv()
    more = [push(far, right, mate, 8)]
    more[0].start()
    sends += more
    for slot, block, cols in (
        (0, mate, whole), (4, obs_of(y - 1, 1 - core), whole), (6, obs_of(y + 1, 1 - core), whole),
        (7, obs_of(y + 2, 1 - core), left), (8, obs_of(y + 2, 1 - core), right),
    ):
        push(block, cols, mate, slot).wait_recv()
    for c in sends:
        c.wait_send()
    save = pltpu.make_async_copy(full, gathered_out, local.at[7])
    save.start()
    for j in range(0, cells, WIDE):
        low[:, j:j + WIDE] = full[:, j:j + WIDE].astype(jnp.bfloat16)

    for c in loads[1:]:
        c.wait()

    def ring_rows(way, step):
        hop = step // 2
        at = lax.rem(z + nz // 2 - hop + nz, nz) if way == 0 else lax.rem(z + nz // 2 + 1 + hop, nz)
        return pl.ds(pl.multiple_of(at * chunk + lax.rem(step, 2) * half, half), half)

    def ring_copy(way, step):
        return pltpu.make_async_remote_copy(
            src_ref=part.at[ring_rows(way, step)], dst_ref=ring_in.at[way, step],
            send_sem=r_send.at[way, step], recv_sem=r_recv.at[way, step],
            device_id={"cell": cell_of(x, z + 1 - 2 * way)}, device_id_type=MESH,
        )

    def column(ref, row, at):
        tile = jnp.broadcast_to(ref[row:row + 1, at], (half, half)).T
        return jnp.concatenate([tile] * (WIDE // LANES), axis=1)

    def compute(step):
        ats = [ring_rows(0, step), ring_rows(1, step)]
        pos_x = jnp.concatenate([column(xy, 0, at) for at in ats], axis=0)
        pos_y = jnp.concatenate([column(xy, 1, at) for at in ats], axis=0)
        height = jnp.concatenate([column(alt, 0, at) for at in ats], axis=0)
        acc = jnp.zeros((chunk, width), jnp.float32)
        for j in range(0, cells, WIDE):
            dx = pos_x - cell_xy[0:1, j:j + WIDE]
            dy = pos_y - cell_xy[1:2, j:j + WIDE]
            h = height + cell_dep[0:1, j:j + WIDE]
            inverse = lax.rsqrt(dx * dx + dy * dy + h * h)
            kernel = ((h * inverse) * (inverse * inverse)).astype(jnp.bfloat16)
            acc += lax.dot_general(
                kernel, low[:, j:j + WIDE], (((1,), (1,)), ((), ())), preferred_element_type=jnp.float32
            )
        part[ats[0], :] = acc[:half]
        part[ats[1], :] = acc[half:]

    def ring_step(step, carry):
        compute(step)

        @pl.when(step > 1)
        def _():
            for way in range(2):
                ring_copy(way, step - 2).wait_recv()
                at = ring_rows(way, step)
                part[at, :] = part[at, :] + ring_in[way, step - 2]

        ring_copy(0, step).start()

        @pl.when(step < nz - 2)
        def _():
            ring_copy(1, step).start()

        return carry

    lax.fori_loop(0, nz, ring_step, 0)
    for step in (nz - 2, nz - 1):
        ring_copy(0, step).wait_recv()
        at = ring_rows(1, step)
        part[at, :] = part[at, :] + ring_in[0, step]

    x_copies = []
    for o in range(1, nx):
        to = lax.rem(x + o, nx)
        x_copies.append(pltpu.make_async_remote_copy(
            src_ref=part.at[pl.ds(pl.multiple_of(z * chunk + to * final, final), final)],
            dst_ref=x_in.at[o - 1], send_sem=x_send.at[o - 1], recv_sem=x_recv.at[o - 1],
            device_id={"cell": cell_of(x + o, z)}, device_id_type=MESH,
        ))
        x_copies[-1].start()
    window = pl.ds(pl.multiple_of(z * chunk + (x // 2) * LANES, LANES), LANES)
    wide_noise[...] = jnp.broadcast_to(noise[0:1, window], (LANES, LANES)).T
    variance = wide_noise[pl.ds(pl.multiple_of(lax.rem(x, 2) * final, final), final), :]
    for c in x_copies:
        c.wait_recv()
    predicted = part[pl.ds(first, final), :]
    for o in range(nx - 1):
        predicted = predicted + x_in[o]
    predicted = predicted * (1.0 / math.sqrt(cells * nx * nz))

    anomaly = predicted - jnp.mean(predicted, axis=1, keepdims=True)
    weighted = anomaly / variance
    rows[0:width, :] = dot32(anomaly, weighted, ((0,), (0,)))
    rows[width:, :] = dot32(tgt[...] - predicted, weighted, ((0,), (0,)))

    thin = rows.shape[0] // (nx * no)
    here = x * no + obs

    def spot(piece):
        return pl.ds(pl.multiple_of(piece * thin, thin), thin)

    def other(o):
        xx, oo = lax.rem(x + o // no, nx), lax.rem(obs + lax.rem(o, no), no)
        return xx * no + oo, {"cell": xx * nz + z, "obs": oo}

    def scatter(o):
        piece, device = other(o)
        return pltpu.make_async_remote_copy(
            src_ref=rows.at[spot(piece)], dst_ref=plane_in.at[o - 1],
            send_sem=a_send.at[o - 1], recv_sem=a_recv.at[o - 1], device_id=device, device_id_type=MESH,
        )

    def along(o):
        return pltpu.make_async_remote_copy(
            src_ref=eighth, dst_ref=z_in.at[o - 1], send_sem=z_send.at[o - 1], recv_sem=z_recv.at[o - 1],
            device_id={"cell": cell_of(x, z + o)}, device_id_type=MESH,
        )

    def gather(o):
        return pltpu.make_async_remote_copy(
            src_ref=total.at[spot(here)], dst_ref=total.at[spot(here)],
            send_sem=b_send.at[o - 1], recv_sem=b_recv.at[o - 1], device_id=other(o)[1], device_id_type=MESH,
        )

    def arrived(o):
        xx, oo = lax.rem(x + nx - o // no, nx), lax.rem(obs + no - lax.rem(o, no), no)
        at = spot(xx * no + oo)
        return pltpu.make_async_remote_copy(
            src_ref=total.at[at], dst_ref=total.at[at],
            send_sem=b_send.at[o - 1], recv_sem=b_recv.at[o - 1], device_id=other(o)[1], device_id_type=MESH,
        )

    def each(count, action):
        lax.fori_loop(1, count, lambda o, carry: (action(o), carry)[1], 0)

    spread = nx * no
    each(spread, lambda o: scatter(o).start())
    each(spread, lambda o: scatter(o).wait_recv())
    eighth[...] = rows[spot(here), :] + jnp.sum(plane_in[...], axis=0)
    each(nz, lambda o: along(o).start())
    each(nz, lambda o: along(o).wait_recv())
    total[spot(here), :] = eighth[...] + jnp.sum(z_in[...], axis=0)
    each(spread, lambda o: gather(o).start())
    each(spread, lambda o: arrived(o).wait_recv())
    gram_out[...] = total[0:width, :]
    cross_out[...] = total[pl.ds(pl.multiple_of(width + obs * mine, mine), mine), :]

    for c in x_copies:
        c.wait_send()
    each(spread, lambda o: scatter(o).wait_send())
    each(nz, lambda o: along(o).wait_send())
    each(spread, lambda o: gather(o).wait_send())

    def drain(step, carry):
        for way in range(2):
            ring_copy(way, step).wait_send()
        return carry

    lax.fori_loop(0, nz - 2, drain, 0)
    for step in (nz - 2, nz - 1):
        ring_copy(0, step).wait_send()
    save.wait()


def pair_inverse(a, b, d):
    scale = 1.0 / (a * d - b * b)
    return d * scale, -b * scale, a * scale


def quad_inverse(d):
    p0, p1, p2 = pair_inverse(d[0][0], d[1][0], d[1][1])
    q = [[d[2][0], d[3][0]], [d[2][1], d[3][1]]]
    u = [[p0 * q[0][j] + p1 * q[1][j] for j in range(2)], [p1 * q[0][j] + p2 * q[1][j] for j in range(2)]]
    s = [[d[2 + i][2 + j] - (q[0][i] * u[0][j] + q[1][i] * u[1][j]) for j in range(i + 1)] for i in range(2)]
    s0, s1, s2 = pair_inverse(s[0][0], s[1][0], s[1][1])
    v = [[u[i][0] * s0 + u[i][1] * s1, u[i][0] * s1 + u[i][1] * s2] for i in range(2)]
    top = [[p0 + v[0][0] * u[0][0] + v[0][1] * u[0][1]],
           [p1 + v[1][0] * u[0][0] + v[1][1] * u[0][1], p2 + v[1][0] * u[1][0] + v[1][1] * u[1][1]]]
    return [
        [top[0][0], top[1][0], -v[0][0], -v[0][1]],
        [top[1][0], top[1][1], -v[1][0], -v[1][1]],
        [-v[0][0], -v[1][0], s0, s1],
        [-v[0][1], -v[1][1], s1, s2],
    ]


def solve_kernel(gram, cross, members, out, full, high, low, sem):
    width, cells = full.shape
    fetch = pltpu.make_async_copy(members, full, sem.at[0])
    fetch.start()
    lane = lax.broadcasted_iota(jnp.int32, (SUB, LANES), 1)
    row = lax.broadcasted_iota(jnp.int32, (SUB, LANES), 0)
    tiles = [
        gram[i:i + SUB, :] + jnp.where(row + i == lane, width - 1.0, 0.0) for i in range(0, width, SUB)
    ]
    tiles += [cross[i:i + SUB, :] for i in range(0, cross.shape[0], SUB)]
    for k in range(0, width, 4):
        live = range((k + 4) // SUB, len(tiles))
        home, base = k // SUB, k % SUB
        pivot = tiles[home]

        def spread(tile, at):
            return jnp.broadcast_to(tile[:, at:at + 1], (SUB, LANES))

        def level(tile, at):
            return jnp.broadcast_to(tile[at:at + 1, :], (SUB, LANES))

        pivot_cols = [spread(pivot, k + j) for j in range(4)]
        block = [[level(pivot_cols[j], base + i) for j in range(i + 1)] for i in range(4)]
        inv = quad_inverse(block)
        steps = [level(pivot, base + i) for i in range(4)]
        moved = []
        for i in range(4):
            t = (inv[i][0] * steps[0] + inv[i][1] * steps[1]) + (inv[i][2] * steps[2] + inv[i][3] * steps[3])
            for m in range(4):
                t = jnp.where(lane == k + m, -inv[i][m], t)
            moved.append(t)
        for n in live:
            cols = pivot_cols if n == home else [spread(tiles[n], k + j) for j in range(4)]
            kept = jnp.where((lane >= k) & (lane < k + 4), 0.0, tiles[n])
            tiles[n] = kept - ((cols[0] * moved[0] + cols[1] * moved[1]) + (cols[2] * moved[2] + cols[3] * moved[3]))
        if k == width // 2:
            fetch.wait()
            for j in range(0, cells, 512):
                value = full[:, j:j + 512]
                top = value.astype(jnp.bfloat16)
                high[:, j:j + 512] = top
                low[:, j:j + 512] = (value - top.astype(jnp.float32)).astype(jnp.bfloat16)
    weights = jnp.concatenate(tiles[width // SUB:], axis=0)
    weights = weights - jnp.mean(weights, axis=1, keepdims=True)
    upper = weights.astype(jnp.bfloat16)
    lower = (weights - upper.astype(jnp.float32)).astype(jnp.bfloat16)
    both = jnp.concatenate([upper, lower], axis=0)
    n = upper.shape[0]
    for j in range(0, cells, 512):
        main = jnp.dot(both, high[:, j:j + 512], preferred_element_type=jnp.float32)
        rest = jnp.dot(upper, low[:, j:j + 512], preferred_element_type=jnp.float32)
        out[:, j:j + 512] = main[:n] + (main[n:] + rest)


def increments(gram, cross, gathered):
    width, cells = gathered.shape
    vmem = pl.BlockSpec(memory_space=pltpu.VMEM)
    return pl.pallas_call(
        solve_kernel,
        out_shape=jax.ShapeDtypeStruct((cross.shape[0], cells), jnp.float32),
        in_specs=[vmem, vmem, pl.BlockSpec(memory_space=pl.ANY)],
        out_specs=vmem,
        scratch_shapes=[
            pltpu.VMEM((width, cells), jnp.float32),
            pltpu.VMEM((width, cells), jnp.bfloat16),
            pltpu.VMEM((width, cells), jnp.bfloat16),
            pltpu.SemaphoreType.DMA((1,)),
        ],
        compiler_params=pltpu.CompilerParams(vmem_limit_bytes=24 * 2**20),
    )(gram, cross, gathered)


def per_device(nx, ny, nz, station_xy, station_alt, cell_xy, cell_depth, members, targets, noise_var):
    own = members.T
    mine, cells = own.shape
    no = 2 * ny
    width = mine * no
    stations = station_alt.shape[0]
    chunk = stations // nz
    half, final = chunk // 2, chunk // nx
    thin = 2 * width // (nx * no)
    f32 = jnp.float32
    vmem = pl.BlockSpec(memory_space=pltpu.VMEM)
    anyw = pl.BlockSpec(memory_space=pl.ANY)
    dma = pltpu.SemaphoreType.DMA
    gathered, gram, cross = pl.pallas_call(
        functools.partial(sums_kernel, nx, ny, nz),
        out_shape=(
            jax.ShapeDtypeStruct((width, cells), f32),
            jax.ShapeDtypeStruct((width, width), f32),
            jax.ShapeDtypeStruct((mine, width), f32),
        ),
        in_specs=[anyw] * 7,
        out_specs=(anyw, vmem, vmem),
        scratch_shapes=[
            pltpu.VMEM((2, stations), f32),
            pltpu.VMEM((1, stations), f32),
            pltpu.VMEM((2, cells), f32),
            pltpu.VMEM((1, cells), f32),
            pltpu.VMEM((1, stations), f32),
            pltpu.VMEM((width, cells), f32),
            pltpu.VMEM((width, cells), jnp.bfloat16),
            pltpu.VMEM((stations, width), f32),
            pltpu.VMEM((2, nz, half, width), f32),
            pltpu.VMEM((nx - 1, final, width), f32),
            pltpu.VMEM((final, width), f32),
            pltpu.VMEM((LANES, LANES), f32),
            pltpu.VMEM((2 * width, width), f32),
            pltpu.VMEM((nx * no - 1, thin, width), f32),
            pltpu.VMEM((thin, width), f32),
            pltpu.VMEM((nz - 1, thin, width), f32),
            pltpu.VMEM((2 * width, width), f32),
            dma((9,)), dma((9,)),
            dma((2, nz)), dma((2, nz)),
            dma((nx - 1,)), dma((nx - 1,)),
            dma((nx * no - 1,)), dma((nx * no - 1,)),
            dma((nz - 1,)), dma((nz - 1,)),
            dma((nx * no - 1,)), dma((nx * no - 1,)),
            dma((8,)),
        ],
        compiler_params=pltpu.CompilerParams(
            collective_id=0, has_side_effects=True, vmem_limit_bytes=48 * 2**20
        ),
    )(station_xy, station_alt[None], cell_xy, cell_depth[None], own, targets, noise_var[None])
    return increments(gram, cross, gathered).T


def solution(mesh):
    nz = 16
    nx = mesh.shape["cell"] // nz
    ny = mesh.shape["obs"] // 2
    placed = (
        P(None, "obs"),
        P("obs"),
        P(None, "cell"),
        P("cell"),
        P("cell", "obs"),
        P("obs", None),
        P("obs"),
    )
    return jax.shard_map(
        functools.partial(per_device, nx, ny, nz),
        mesh=mesh, in_specs=placed, out_specs=P("cell", "obs"), check_vma=False,
    )
```

time: 154 us -> 105 us (0.68)
  other arithmetic: 22.9 us -> 0 us
  Pallas kernels: 121 us -> 98.4 us
  matrix products: 2.55 us -> 0 us
    pallas_call x1, Pallas kernels: 121 us -> 91.6 us  [per_device(): pl.pallas_call(functools.partial(sums_kernel, nx, ny, nz), out_shape=(jax...]
    another operation x5 -> x0, other arithmetic: 22.9 us -> none  [the longest x3 12.4 us: per_device(): factor = jnp.linalg.cholesky(matrix)]
    pallas_call x0 -> x1, Pallas kernels: none -> 6.74 us  [increments(): pl.pallas_call(solve_kernel, out_shape=jax.ShapeDtypeStruct((cross.shape[...]
    dot_general x1 -> x0, matrix products: 1.91 us -> none  [per_device(): return jnp.dot(gathered.T, coeffs, precision=lax.Precision.HIGHEST)]
where the time goes in v2:
time: 105 us
  Pallas kernels  98.4 us (94%)
  local copies, waits for them, and re-layouts  6.21 us (6%)
    pallas_call x1, Pallas kernels, per_device(): pl.pallas_call(functools.partial(sums_kernel, nx, ny, nz), out_shape=(jax...  91.6 us
    pallas_call x1, Pallas kernels, increments(): pl.pallas_call(solve_kernel, out_shape=jax.ShapeDtypeStruct((cross.shape[...  6.74 us
    unnamed x14, local copies, waits for them, and re-layouts  6.21 us

profile of v2, /device:TPU:1, one launch (start us, length us, event | category | flops | bytes accessed | tf_op | source)
XLA Modules:
  0.0 104.6 jit_solution(7400697320079635355)
XLA Ops:
  0.0 0.0 copy-start
  0.0 1.6 %copy-done = f32[4096,128]{1,0:T(8,128)S(1)} copy-done((f32[4096,128]{1,0:T(8,128)S(1)}, f32[4096,128]{1,0:T(8,128)}, u32[]{:S(2)}) %copy-start) | copy-done | bytes 2097176
  1.6 0.0 copy-start.1
  1.6 0.9 copy-done.1
  2.5 0.0 copy-start.2
  2.5 0.8 copy-done.2
  3.3 0.0 copy-start.3
  3.3 0.8 copy-done.3
  4.1 0.0 copy-start.4
  4.1 0.7 copy-done.4
  4.8 0.0 copy-start.5
  4.8 0.7 copy-done.5
  5.5 0.0 copy-start.6
  5.5 0.7 copy-done.6
  6.2 91.6 %shard_map.73 = (f32[128,4096]{1,0:T(8,128)S(1)}, f32[128,128]{1,0:T(8,128)S(1)}, f32[16,128]{1,0:T(8,128)S(1)}) custom-call(f32[2,4096]{1,0:T(2,128)S(1)} %copy-done.2, f32[1,4096]{1,0:T(1,128)S(1)} %bitcast.6, f32[2,4096]{1,0:T(2,128)S(1)} %copy-done.3, f32[1,4096]{1,0:T(1,128)S(1)} %bitcast.7, f32[16,4096]{1,0:T(8,128)S(1)} %bitcast.5, ...), custom_call_target="tpu_custom_call" | custom-call | tf_op jit(solution)/shard_map/pallas_call | solution.py:373
  97.9 6.7 %shard_map.74 = f32[16,4096]{1,0:T(8,128)} custom-call(f32[128,128]{1,0:T(8,128)S(1)} %get-tuple-element.8.gram, f32[16,128]{1,0:T(8,128)S(1)} %get-tuple-element.9.cross, f32[128,4096]{1,0:T(8,128)S(1)} %get-tuple-element.10.members), custom_call_target="tpu_custom_call" | custom-call | tf_op jit(solution)/shard_map/pallas_call | solution.py:345
Async XLA Ops:
  0.0 1.6 %copy-start = (f32[4096,128]{1,0:T(8,128)S(1)}, f32[4096,128]{1,0:T(8,128)}, u32[]{:S(2)}) copy-start(f32[4096,128]{1,0:T(8,128)} %targets.1) | copy-start | bytes 6291460
  1.6 0.9 copy-start.1
  2.5 0.8 copy-start.2
  3.3 0.8 copy-start.3
  4.1 0.7 copy-start.4
  4.8 0.7 copy-start.5
  5.5 0.7 copy-start.6

commit v3 on v2

--- a/solution.py
+++ b/solution.py
@@ -12,6 +12,8 @@
 SUB = 8
 LANES = 128
 WIDE = 512
+AHEAD = (1, 3, 4, 5, 5)
+CUTS = 1
 
 
 def dot32(a, b, dims):
@@ -21,9 +23,9 @@
 
 
 def sums_kernel(nx, ny, nz, xy_in, alt_in, cell_xy_in, cell_dep_in, own, targets, noise_in,
-                gathered_out, gram_out, cross_out,
+                high_out, low_out, gram_out, cross_out,
                 xy, alt, cell_xy, cell_dep, noise,
-                full, low, part, ring_in, x_in, tgt, wide_noise, rows, plane_in, eighth, z_in, total,
+                full, low, rest, ahead, part, ring_in, x_in, tgt, wide_noise, rows, plane_in, eighth, z_in, total,
                 g_send, g_recv, r_send, r_recv, x_send, x_recv, a_send, a_recv,
                 z_send, z_recv, b_send, b_recv, local):
     obs, cell = lax.axis_index("obs"), lax.axis_index("cell")
@@ -60,56 +62,7 @@
     ]
     for c in loads:
         c.start()
-    loads[0].wait()
-    pl.semaphore_wait(barrier, len(peers))
-
-    cut = cells // 2
-    left, right, whole = pl.ds(0, cut), pl.ds(cut, cut), pl.ds(0, cells)
-
-    def push(block, cols, target, slot):
-        at = pl.ds(pl.multiple_of(block * mine, mine), mine)
-        return pltpu.make_async_remote_copy(
-            src_ref=full.at[at, cols], dst_ref=full.at[at, cols],
-            send_sem=g_send.at[slot], recv_sem=g_recv.at[slot],
-            device_id={"obs": target}, device_id_type=MESH,
-        )
-
-    mate, up, down = obs_of(y, 1 - core), obs_of(y + 1, core), obs_of(y - 1, core)
-    far = obs_of(y + 2, core)
-    sends = [push(obs, whole, mate, 0), push(obs, whole, up, 1), push(obs, whole, down, 2)]
-    for c in sends:
-        c.start()
-    push(down, whole, up, 1).wait_recv()
-    more = [push(down, left, up, 3), push(down, whole, mate, 4)]
-    for c in more:
-        c.start()
-    sends += more
-    push(up, whole, down, 2).wait_recv()
-    more = [push(up, right, down, 5), push(up, whole, mate, 6)]
-    for c in more:
-        c.start()
-    sends += more
-    push(far, left, up, 3).wait_recv()
-    more = [push(far, left, mate, 7)]
-    more[0].start()
-    sends += more
-    push(far, right, down, 5).wait_recv()
-    more = [push(far, right, mate, 8)]
-    more[0].start()
-    sends += more
-    for slot, block, cols in (
-        (0, mate, whole), (4, obs_of(y - 1, 1 - core), whole), (6, obs_of(y + 1, 1 - core), whole),
-        (7, obs_of(y + 2, 1 - core), left), (8, obs_of(y + 2, 1 - core), right),
-    ):
-        push(block, cols, mate, slot).wait_recv()
-    for c in sends:
-        c.wait_send()
-    save = pltpu.make_async_copy(full, gathered_out, local.at[7])
-    save.start()
-    for j in range(0, cells, WIDE):
-        low[:, j:j + WIDE] = full[:, j:j + WIDE].astype(jnp.bfloat16)
-
-    for c in loads[1:]:
+    for c in loads:
         c.wait()
 
     def ring_rows(way, step):
@@ -117,61 +70,147 @@
         at = lax.rem(z + nz // 2 - hop + nz, nz) if way == 0 else lax.rem(z + nz // 2 + 1 + hop, nz)
         return pl.ds(pl.multiple_of(at * chunk + lax.rem(step, 2) * half, half), half)
 
-    def ring_copy(way, step):
-        return pltpu.make_async_remote_copy(
-            src_ref=part.at[ring_rows(way, step)], dst_ref=ring_in.at[way, step],
-            send_sem=r_send.at[way, step], recv_sem=r_recv.at[way, step],
-            device_id={"cell": cell_of(x, z + 1 - 2 * way)}, device_id_type=MESH,
-        )
-
     def column(ref, row, at):
         tile = jnp.broadcast_to(ref[row:row + 1, at], (half, half)).T
         return jnp.concatenate([tile] * (WIDE // LANES), axis=1)
 
-    def compute(step):
+    def places(step):
         ats = [ring_rows(0, step), ring_rows(1, step)]
-        pos_x = jnp.concatenate([column(xy, 0, at) for at in ats], axis=0)
-        pos_y = jnp.concatenate([column(xy, 1, at) for at in ats], axis=0)
-        height = jnp.concatenate([column(alt, 0, at) for at in ats], axis=0)
+        return [jnp.concatenate([column(ref, row, at) for at in ats], axis=0) for ref, row in ((xy, 0), (xy, 1), (alt, 0))]
+
+    def kernel_of(place, j):
+        dx = place[0] - cell_xy[0:1, j:j + WIDE]
+        dy = place[1] - cell_xy[1:2, j:j + WIDE]
+        h = place[2] + cell_dep[0:1, j:j + WIDE]
+        inverse = lax.rsqrt(dx * dx + dy * dy + h * h)
+        return ((h * inverse) * (inverse * inverse)).astype(jnp.bfloat16)
+
+    def times_members(kernel, j):
+        return lax.dot_general(
+            kernel, low[:, j:j + WIDE], (((1,), (1,)), ((), ())), preferred_element_type=jnp.float32
+        )
+
+    cut = cells // 2
+    left, right, whole = pl.ds(0, cut), pl.ds(cut, cut), pl.ds(0, cells)
+
+    def push(block, cols, target, slot):
+        at = pl.ds(pl.multiple_of(block * mine, mine), mine)
+        return pltpu.make_async_remote_copy(
+            src_ref=full.at[at, cols], dst_ref=full.at[at, cols],
+            send_sem=g_send.at[slot], recv_sem=g_recv.at[slot],
+            device_id={"obs": target}, device_id_type=MESH,
+        )
+
+    mate, up, down = obs_of(y, 1 - core), obs_of(y + 1, core), obs_of(y - 1, core)
+    far = obs_of(y + 2, core)
+    own_up = [push(obs, left, up, 1), push(obs, right, up, 2)]
+    own_down = [push(obs, right, down, 3), push(obs, left, down, 4)]
+    pass_up, pass_down = push(down, left, up, 5), push(up, right, down, 6)
+    to_mate = [
+        push(obs, whole, mate, 0), push(down, whole, mate, 7), push(up, whole, mate, 8),
+        push(far, left, mate, 9), push(far, right, mate, 10),
+    ]
+    sends = own_up + own_down + [pass_up, pass_down] + to_mate
+
+    def build(step, carry):
+        place = places(step)
+        for j in range(0, cells, WIDE):
+            ahead[step, :, j:j + WIDE] = kernel_of(place, j)
+
+        @pl.when(step == AHEAD[0] - 1)
+        def _():
+            pl.semaphore_wait(barrier, len(peers))
+            for c in (own_up[0], own_down[0], own_up[1], own_down[1], to_mate[0]):
+                c.start()
+
+        @pl.when(step == AHEAD[1] - 1)
+        def _():
+            push(down, left, up, 1).wait_recv()
+            push(up, right, down, 3).wait_recv()
+            pass_up.start()
+            pass_down.start()
+
+        @pl.when(step == AHEAD[2] - 1)
+        def _():
+            push(down, right, up, 2).wait_recv()
+            push(up, left, down, 4).wait_recv()
+            to_mate[1].start()
+            to_mate[2].start()
+
+        @pl.when(step == AHEAD[3] - 1)
+        def _():
+            push(far, left, up, 5).wait_recv()
+            push(far, right, down, 6).wait_recv()
+            to_mate[3].start()
+            to_mate[4].start()
+
+        return carry
+
+    lax.fori_loop(0, AHEAD[-1], build, 0)
+    for slot, block, cols in (
+        (0, mate, whole), (7, obs_of(y - 1, 1 - core), whole), (8, obs_of(y + 1, 1 - core), whole),
+        (9, obs_of(y + 2, 1 - core), left), (10, obs_of(y + 2, 1 - core), right),
+    ):
+        push(block, cols, mate, slot).wait_recv()
+    for j in range(0, cells, WIDE):
+        low[:, j:j + WIDE] = full[:, j:j + WIDE].astype(jnp.bfloat16)
+    saves = [pltpu.make_async_copy(low, high_out, local.at[7]), pltpu.make_async_copy(rest, low_out, local.at[8])]
+    saves[0].start()
+
+    def ring_rows_of(way, step, piece):
+        rows_at = ring_rows(way, step)
+        return pl.ds(pl.multiple_of(rows_at.start + piece * (half // CUTS), half // CUTS), half // CUTS)
+
+    def ring_copy(way, step, piece):
+        return pltpu.make_async_remote_copy(
+            src_ref=part.at[ring_rows_of(way, step, piece)],
+            dst_ref=ring_in.at[way, step, pl.ds(piece * (half // CUTS), half // CUTS)],
+            send_sem=r_send.at[way, step, piece], recv_sem=r_recv.at[way, step, piece],
+            device_id={"cell": cell_of(x, z + 1 - 2 * way)}, device_id_type=MESH,
+        )
+
+    def take(way, step, target, piece):
+        ring_copy(way, step, piece).wait_recv()
+        at = ring_rows_of(target[0], target[1], piece)
+        part[at, :] = part[at, :] + ring_in[way, step, pl.ds(piece * (half // CUTS), half // CUTS)]
+
+    def ring_step(step, kernels):
         acc = jnp.zeros((chunk, width), jnp.float32)
         for j in range(0, cells, WIDE):
-            dx = pos_x - cell_xy[0:1, j:j + WIDE]
-            dy = pos_y - cell_xy[1:2, j:j + WIDE]
-            h = height + cell_dep[0:1, j:j + WIDE]
-            inverse = lax.rsqrt(dx * dx + dy * dy + h * h)
-            kernel = ((h * inverse) * (inverse * inverse)).astype(jnp.bfloat16)
-            acc += lax.dot_general(
-                kernel, low[:, j:j + WIDE], (((1,), (1,)), ((), ())), preferred_element_type=jnp.float32
-            )
-        part[ats[0], :] = acc[:half]
-        part[ats[1], :] = acc[half:]
-
-    def ring_step(step, carry):
-        compute(step)
-
-        @pl.when(step > 1)
-        def _():
+            acc += times_members(kernels(j), j)
+        part[ring_rows(0, step), :] = acc[:half]
+        part[ring_rows(1, step), :] = acc[half:]
+
+        for piece in range(CUTS):
             for way in range(2):
-                ring_copy(way, step - 2).wait_recv()
-                at = ring_rows(way, step)
-                part[at, :] = part[at, :] + ring_in[way, step - 2]
-
-        ring_copy(0, step).start()
-
-        @pl.when(step < nz - 2)
-        def _():
-            ring_copy(1, step).start()
-
+                @pl.when(step > 1)
+                def _():
+                    take(way, step - 2, (way, step), piece)
+
+                if way == 0:
+                    ring_copy(0, step, piece).start()
+                else:
+                    @pl.when(step < nz - 2)
+                    def _():
+                        ring_copy(1, step, piece).start()
+
+    def built_step(step, carry):
+        ring_step(step, lambda j: ahead[step, :, j:j + WIDE])
         return carry
 
-    lax.fori_loop(0, nz, ring_step, 0)
+    def fresh_step(step, carry):
+        place = places(step)
+        ring_step(step, lambda j: kernel_of(place, j))
+        return carry
+
+    lax.fori_loop(0, AHEAD[-1], built_step, 0)
+    lax.fori_loop(AHEAD[-1], nz, fresh_step, 0)
     for step in (nz - 2, nz - 1):
-        ring_copy(0, step).wait_recv()
-        at = ring_rows(1, step)
-        part[at, :] = part[at, :] + ring_in[0, step]
+        for piece in range(CUTS):
+            take(0, step, (1, step), piece)
 
     x_copies = []
-    for o in range(1, nx):
+    for o in sorted(range(1, nx), key=lambda o: abs(o - nx // 2)):
         to = lax.rem(x + o, nx)
         x_copies.append(pltpu.make_async_remote_copy(
             src_ref=part.at[pl.ds(pl.multiple_of(z * chunk + to * final, final), final)],
@@ -231,36 +270,56 @@
             send_sem=b_send.at[o - 1], recv_sem=b_recv.at[o - 1], device_id=other(o)[1], device_id_type=MESH,
         )
 
-    def each(count, action):
-        lax.fori_loop(1, count, lambda o, carry: (action(o), carry)[1], 0)
-
-    spread = nx * no
-    each(spread, lambda o: scatter(o).start())
-    each(spread, lambda o: scatter(o).wait_recv())
+    def fan(i, middle):
+        return middle + ((i + 1) // 2) * (1 - 2 * lax.rem(i, 2))
+
+    def over_plane(action):
+        def one(i, carry):
+            action(fan(i // no, nx // 2) * no + fan(lax.rem(i, no), no // 2))
+            return carry
+
+        lax.fori_loop(0, nx * no - 1, one, 0)
+
+    def over_z(action):
+        def one(i, carry):
+            action(fan(i, nz // 2))
+            return carry
+
+        lax.fori_loop(0, nz - 1, one, 0)
+
+    over_plane(lambda o: scatter(o).start())
+    for j in range(0, cells, WIDE):
+        exact = full[:, j:j + WIDE]
+        rest[:, j:j + WIDE] = (exact - low[:, j:j + WIDE].astype(jnp.float32)).astype(jnp.bfloat16)
+    saves[1].start()
+    over_plane(lambda o: scatter(o).wait_recv())
     eighth[...] = rows[spot(here), :] + jnp.sum(plane_in[...], axis=0)
-    each(nz, lambda o: along(o).start())
-    each(nz, lambda o: along(o).wait_recv())
+    over_z(lambda o: along(o).start())
+    for c in sends + x_copies:
+        c.wait_send()
+
+    def drain(step, carry):
+        for piece in range(CUTS):
+            ring_copy(0, step, piece).wait_send()
+
+            @pl.when(step < nz - 2)
+            def _():
+                ring_copy(1, step, piece).wait_send()
+
+        return carry
+
+    lax.fori_loop(0, nz, drain, 0)
+    over_plane(lambda o: scatter(o).wait_send())
+    over_z(lambda o: along(o).wait_recv())
     total[spot(here), :] = eighth[...] + jnp.sum(z_in[...], axis=0)
-    each(spread, lambda o: gather(o).start())
-    each(spread, lambda o: arrived(o).wait_recv())
+    over_plane(lambda o: gather(o).start())
+    over_z(lambda o: along(o).wait_send())
+    for c in saves:
+        c.wait()
+    over_plane(lambda o: arrived(o).wait_recv())
     gram_out[...] = total[0:width, :]
     cross_out[...] = total[pl.ds(pl.multiple_of(width + obs * mine, mine), mine), :]
-
-    for c in x_copies:
-        c.wait_send()
-    each(spread, lambda o: scatter(o).wait_send())
-    each(nz, lambda o: along(o).wait_send())
-    each(spread, lambda o: gather(o).wait_send())
-
-    def drain(step, carry):
-        for way in range(2):
-            ring_copy(way, step).wait_send()
-        return carry
-
-    lax.fori_loop(0, nz - 2, drain, 0)
-    for step in (nz - 2, nz - 1):
-        ring_copy(0, step).wait_send()
-    save.wait()
+    over_plane(lambda o: gather(o).wait_send())
 
 
 def pair_inverse(a, b, d):
@@ -285,10 +344,11 @@
     ]
 
 
-def solve_kernel(gram, cross, members, out, full, high, low, sem):
-    width, cells = full.shape
-    fetch = pltpu.make_async_copy(members, full, sem.at[0])
-    fetch.start()
+def solve_kernel(gram, cross, high_in, low_in, out, high, low, sem):
+    width, cells = high.shape
+    fetches = [pltpu.make_async_copy(high_in, high, sem.at[0]), pltpu.make_async_copy(low_in, low, sem.at[1])]
+    for c in fetches:
+        c.start()
     lane = lax.broadcasted_iota(jnp.int32, (SUB, LANES), 1)
     row = lax.broadcasted_iota(jnp.int32, (SUB, LANES), 0)
     tiles = [
@@ -320,18 +380,13 @@
             cols = pivot_cols if n == home else [spread(tiles[n], k + j) for j in range(4)]
             kept = jnp.where((lane >= k) & (lane < k + 4), 0.0, tiles[n])
             tiles[n] = kept - ((cols[0] * moved[0] + cols[1] * moved[1]) + (cols[2] * moved[2] + cols[3] * moved[3]))
-        if k == width // 2:
-            fetch.wait()
-            for j in range(0, cells, 512):
-                value = full[:, j:j + 512]
-                top = value.astype(jnp.bfloat16)
-                high[:, j:j + 512] = top
-                low[:, j:j + 512] = (value - top.astype(jnp.float32)).astype(jnp.bfloat16)
     weights = jnp.concatenate(tiles[width // SUB:], axis=0)
     weights = weights - jnp.mean(weights, axis=1, keepdims=True)
     upper = weights.astype(jnp.bfloat16)
     lower = (weights - upper.astype(jnp.float32)).astype(jnp.bfloat16)
     both = jnp.concatenate([upper, lower], axis=0)
+    for c in fetches:
+        c.wait()
     n = upper.shape[0]
     for j in range(0, cells, 512):
         main = jnp.dot(both, high[:, j:j + 512], preferred_element_type=jnp.float32)
@@ -339,22 +394,21 @@
         out[:, j:j + 512] = main[:n] + (main[n:] + rest)
 
 
-def increments(gram, cross, gathered):
-    width, cells = gathered.shape
+def increments(gram, cross, high, low):
+    width, cells = high.shape
     vmem = pl.BlockSpec(memory_space=pltpu.VMEM)
     return pl.pallas_call(
         solve_kernel,
         out_shape=jax.ShapeDtypeStruct((cross.shape[0], cells), jnp.float32),
-        in_specs=[vmem, vmem, pl.BlockSpec(memory_space=pl.ANY)],
+        in_specs=[vmem, vmem, pl.BlockSpec(memory_space=pl.ANY), pl.BlockSpec(memory_space=pl.ANY)],
         out_specs=vmem,
         scratch_shapes=[
-            pltpu.VMEM((width, cells), jnp.float32),
             pltpu.VMEM((width, cells), jnp.bfloat16),
             pltpu.VMEM((width, cells), jnp.bfloat16),
-            pltpu.SemaphoreType.DMA((1,)),
+            pltpu.SemaphoreType.DMA((2,)),
         ],
-        compiler_params=pltpu.CompilerParams(vmem_limit_bytes=24 * 2**20),
-    )(gram, cross, gathered)
+        compiler_params=pltpu.CompilerParams(vmem_limit_bytes=64 * 2**20),
+    )(gram, cross, high, low)
 
 
 def per_device(nx, ny, nz, station_xy, station_alt, cell_xy, cell_depth, members, targets, noise_var):
@@ -370,15 +424,16 @@
     vmem = pl.BlockSpec(memory_space=pltpu.VMEM)
     anyw = pl.BlockSpec(memory_space=pl.ANY)
     dma = pltpu.SemaphoreType.DMA
-    gathered, gram, cross = pl.pallas_call(
+    high, low, gram, cross = pl.pallas_call(
         functools.partial(sums_kernel, nx, ny, nz),
         out_shape=(
-            jax.ShapeDtypeStruct((width, cells), f32),
+            jax.ShapeDtypeStruct((width, cells), jnp.bfloat16),
+            jax.ShapeDtypeStruct((width, cells), jnp.bfloat16),
             jax.ShapeDtypeStruct((width, width), f32),
             jax.ShapeDtypeStruct((mine, width), f32),
         ),
-        in_specs=[anyw] * 7,
-        out_specs=(anyw, vmem, vmem),
+        in_specs=[pl.BlockSpec(memory_space=pltpu.HBM)] * 7,
+        out_specs=(anyw, anyw, vmem, vmem),
         scratch_shapes=[
             pltpu.VMEM((2, stations), f32),
             pltpu.VMEM((1, stations), f32),
@@ -387,6 +442,8 @@
             pltpu.VMEM((1, stations), f32),
             pltpu.VMEM((width, cells), f32),
             pltpu.VMEM((width, cells), jnp.bfloat16),
+            pltpu.VMEM((width, cells), jnp.bfloat16),
+            pltpu.VMEM((AHEAD[-1], chunk, cells), jnp.bfloat16),
             pltpu.VMEM((stations, width), f32),
             pltpu.VMEM((2, nz, half, width), f32),
             pltpu.VMEM((nx - 1, final, width), f32),
@@ -397,19 +454,19 @@
             pltpu.VMEM((thin, width), f32),
             pltpu.VMEM((nz - 1, thin, width), f32),
             pltpu.VMEM((2 * width, width), f32),
-            dma((9,)), dma((9,)),
-            dma((2, nz)), dma((2, nz)),
+            dma((11,)), dma((11,)),
+            dma((2, nz, CUTS)), dma((2, nz, CUTS)),
             dma((nx - 1,)), dma((nx - 1,)),
             dma((nx * no - 1,)), dma((nx * no - 1,)),
             dma((nz - 1,)), dma((nz - 1,)),
             dma((nx * no - 1,)), dma((nx * no - 1,)),
-            dma((8,)),
+            dma((9,)),
         ],
         compiler_params=pltpu.CompilerParams(
-            collective_id=0, has_side_effects=True, vmem_limit_bytes=48 * 2**20
+            collective_id=0, has_side_effects=True, vmem_limit_bytes=64 * 2**20
         ),
     )(station_xy, station_alt[None], cell_xy, cell_depth[None], own, targets, noise_var[None])
-    return increments(gram, cross, gathered).T
+    return increments(gram, cross, high, low).T
 
 
 def solution(mesh):

time: 105 us -> 101 us (0.962)
  local copies, waits for them, and re-layouts: 6.21 us -> 0 us
  Pallas kernels: 98.4 us -> 100 us
    unnamed x14 -> x0, local copies, waits for them, and re-layouts: 6.21 us -> none
    pallas_call x1, Pallas kernels: 6.74 us -> 9.52 us  [increments(): pl.pallas_call(solve_kernel, out_shape=jax.ShapeDtypeStruct((cross.shape[...]
where the time goes in v3:
time: 101 us; the launch traced here: 100 us
  Pallas kernels  100 us (99%)
    pallas_call x1, Pallas kernels, per_device(): pl.pallas_call(functools.partial(sums_kernel, nx, ny, nz), out_shape=(jax...  90.8 us
    pallas_call x1, Pallas kernels, increments(): pl.pallas_call(solve_kernel, out_shape=jax.ShapeDtypeStruct((cross.shape[...  9.52 us

profile of v3, /device:TPU:1, one launch (start us, length us, event | category | flops | bytes accessed | tf_op | source)
XLA Modules:
  0.0 100.3 jit_solution(8215095493756730311)
XLA Ops:
  0.0 90.8 %shard_map.73 = (bf16[128,4096]{1,0:T(8,128)(2,1)}, bf16[128,4096]{1,0:T(8,128)(2,1)}, f32[128,128]{1,0:T(8,128)}, f32[16,128]{1,0:T(8,128)}) custom-call(f32[2,4096]{1,0:T(2,128)} %xy_in.1, f32[1,4096]{1,0:T(1,128)} %bitcast.6, f32[2,4096]{1,0:T(2,128)} %cell_xy_in.1, f32[1,4096]{1,0:T(1,128)} %bitcast.7, f32[16,4096]{1,0:T(8,128)} %bitcast.5, ...), custom_call_target="tpu_custom_call" | custom-call | tf_op jit(solution)/shard_map/pallas_call | solution.py:427
  90.8 9.5 %shard_map.74 = f32[16,4096]{1,0:T(8,128)} custom-call(f32[128,128]{1,0:T(8,128)} %get-tuple-element.9.gram, f32[16,128]{1,0:T(8,128)} %get-tuple-element.10.cross, bf16[128,4096]{1,0:T(8,128)(2,1)} %get-tuple-element.11.high_in, bf16[128,4096]{1,0:T(8,128)(2,1)} %get-tuple-element.12.low_in), custom_call_target="tpu_custom_call" | custom-call | tf_op jit(solution)/shard_map/pallas_call | solution.py:400

commit v4 on v3

--- a/solution.py
+++ b/solution.py
@@ -12,7 +12,8 @@
 SUB = 8
 LANES = 128
 WIDE = 512
-AHEAD = (1, 3, 4, 5, 5)
+AHEAD = (2, 2, 2, 2)
+PAIR = 2
 CUTS = 1
 
 
@@ -22,8 +23,66 @@
     )
 
 
+def pair_inverse(a, b, d):
+    scale = 1.0 / (a * d - b * b)
+    return d * scale, -b * scale, a * scale
+
+
+def quad_inverse(d):
+    p0, p1, p2 = pair_inverse(d[0][0], d[1][0], d[1][1])
+    q = [[d[2][0], d[3][0]], [d[2][1], d[3][1]]]
+    u = [[p0 * q[0][j] + p1 * q[1][j] for j in range(2)], [p1 * q[0][j] + p2 * q[1][j] for j in range(2)]]
+    s = [[d[2 + i][2 + j] - (q[0][i] * u[0][j] + q[1][i] * u[1][j]) for j in range(i + 1)] for i in range(2)]
+    s0, s1, s2 = pair_inverse(s[0][0], s[1][0], s[1][1])
+    v = [[u[i][0] * s0 + u[i][1] * s1, u[i][0] * s1 + u[i][1] * s2] for i in range(2)]
+    top = [[p0 + v[0][0] * u[0][0] + v[0][1] * u[0][1]],
+           [p1 + v[1][0] * u[0][0] + v[1][1] * u[0][1], p2 + v[1][0] * u[1][0] + v[1][1] * u[1][1]]]
+    return [
+        [top[0][0], top[1][0], -v[0][0], -v[0][1]],
+        [top[1][0], top[1][1], -v[1][0], -v[1][1]],
+        [-v[0][0], -v[1][0], s0, s1],
+        [-v[0][1], -v[1][1], s1, s2],
+    ]
+
+
+def solve_rows(gram, cross):
+    width = SUB * len(gram)
+    lane = lax.broadcasted_iota(jnp.int32, (SUB, LANES), 1)
+    row = lax.broadcasted_iota(jnp.int32, (SUB, LANES), 0)
+    tiles = [
+        gram[i // SUB] + jnp.where(row + i == lane, width - 1.0, 0.0) for i in range(0, width, SUB)
+    ]
+    tiles += [cross[i:i + SUB] for i in range(0, cross.shape[0], SUB)]
+    for k in range(0, width, 4):
+        live = range((k + 4) // SUB, len(tiles))
+        home, base = k // SUB, k % SUB
+        pivot = tiles[home]
+
+        def spread(tile, at):
+            return jnp.broadcast_to(tile[:, at:at + 1], (SUB, LANES))
+
+        def level(tile, at):
+            return jnp.broadcast_to(tile[at:at + 1, :], (SUB, LANES))
+
+        pivot_cols = [spread(pivot, k + j) for j in range(4)]
+        block = [[level(pivot_cols[j], base + i) for j in range(i + 1)] for i in range(4)]
+        inv = quad_inverse(block)
+        steps = [level(pivot, base + i) for i in range(4)]
+        moved = []
+        for i in range(4):
+            t = (inv[i][0] * steps[0] + inv[i][1] * steps[1]) + (inv[i][2] * steps[2] + inv[i][3] * steps[3])
+            for m in range(4):
+                t = jnp.where(lane == k + m, -inv[i][m], t)
+            moved.append(t)
+        for n in live:
+            cols = pivot_cols if n == home else [spread(tiles[n], k + j) for j in range(4)]
+            kept = jnp.where((lane >= k) & (lane < k + 4), 0.0, tiles[n])
+            tiles[n] = kept - ((cols[0] * moved[0] + cols[1] * moved[1]) + (cols[2] * moved[2] + cols[3] * moved[3]))
+    return jnp.concatenate(tiles[width // SUB:], axis=0)
+
+
 def sums_kernel(nx, ny, nz, xy_in, alt_in, cell_xy_in, cell_dep_in, own, targets, noise_in,
-                high_out, low_out, gram_out, cross_out,
+                out,
                 xy, alt, cell_xy, cell_dep, noise,
                 full, low, rest, ahead, part, ring_in, x_in, tgt, wide_noise, rows, plane_in, eighth, z_in, total,
                 g_send, g_recv, r_send, r_recv, x_send, x_recv, a_send, a_recv,
@@ -62,12 +121,9 @@
     ]
     for c in loads:
         c.start()
-    for c in loads:
-        c.wait()
-
     def ring_rows(way, step):
         hop = step // 2
-        at = lax.rem(z + nz // 2 - hop + nz, nz) if way == 0 else lax.rem(z + nz // 2 + 1 + hop, nz)
+        at = lax.rem(z + nz + nz // 2 - hop + way * (1 + 2 * hop), nz)
         return pl.ds(pl.multiple_of(at * chunk + lax.rem(step, 2) * half, half), half)
 
     def column(ref, row, at):
@@ -75,7 +131,9 @@
         return jnp.concatenate([tile] * (WIDE // LANES), axis=1)
 
     def places(step):
-        ats = [ring_rows(0, step), ring_rows(1, step)]
+        return places_at([ring_rows(0, step), ring_rows(1, step)])
+
+    def places_at(ats):
         return [jnp.concatenate([column(ref, row, at) for at in ats], axis=0) for ref, row in ((xy, 0), (xy, 1), (alt, 0))]
 
     def kernel_of(place, j):
@@ -103,14 +161,27 @@
 
     mate, up, down = obs_of(y, 1 - core), obs_of(y + 1, core), obs_of(y - 1, core)
     far = obs_of(y + 2, core)
-    own_up = [push(obs, left, up, 1), push(obs, right, up, 2)]
-    own_down = [push(obs, right, down, 3), push(obs, left, down, 4)]
+    def push_own(cols, target, slot):
+        return pltpu.make_async_remote_copy(
+            src_ref=own.at[:, cols], dst_ref=full.at[mine_rows, cols],
+            send_sem=g_send.at[slot], recv_sem=g_recv.at[slot],
+            device_id={"obs": target}, device_id_type=MESH,
+        )
+
+    own_up = [push_own(left, up, 1), push_own(right, up, 2)]
+    own_down = [push_own(right, down, 3), push_own(left, down, 4)]
     pass_up, pass_down = push(down, left, up, 5), push(up, right, down, 6)
     to_mate = [
-        push(obs, whole, mate, 0), push(down, whole, mate, 7), push(up, whole, mate, 8),
+        push_own(whole, mate, 0), push(down, whole, mate, 7), push(up, whole, mate, 8),
         push(far, left, mate, 9), push(far, right, mate, 10),
     ]
     sends = own_up + own_down + [pass_up, pass_down] + to_mate
+
+    pl.semaphore_wait(barrier, len(peers))
+    for c in (own_up[0], own_down[0], own_up[1], own_down[1], to_mate[0]):
+        c.start()
+    for c in loads:
+        c.wait()
 
     def build(step, carry):
         place = places(step)
@@ -118,26 +189,20 @@
             ahead[step, :, j:j + WIDE] = kernel_of(place, j)
 
         @pl.when(step == AHEAD[0] - 1)
-        def _():
-            pl.semaphore_wait(barrier, len(peers))
-            for c in (own_up[0], own_down[0], own_up[1], own_down[1], to_mate[0]):
-                c.start()
-
-        @pl.when(step == AHEAD[1] - 1)
         def _():
             push(down, left, up, 1).wait_recv()
             push(up, right, down, 3).wait_recv()
             pass_up.start()
             pass_down.start()
 
-        @pl.when(step == AHEAD[2] - 1)
+        @pl.when(step == AHEAD[1] - 1)
         def _():
             push(down, right, up, 2).wait_recv()
             push(up, left, down, 4).wait_recv()
             to_mate[1].start()
             to_mate[2].start()
 
-        @pl.when(step == AHEAD[3] - 1)
+        @pl.when(step == AHEAD[2] - 1)
         def _():
             push(far, left, up, 5).wait_recv()
             push(far, right, down, 6).wait_recv()
@@ -154,8 +219,6 @@
         push(block, cols, mate, slot).wait_recv()
     for j in range(0, cells, WIDE):
         low[:, j:j + WIDE] = full[:, j:j + WIDE].astype(jnp.bfloat16)
-    saves = [pltpu.make_async_copy(low, high_out, local.at[7]), pltpu.make_async_copy(rest, low_out, local.at[8])]
-    saves[0].start()
 
     def ring_rows_of(way, step, piece):
         rows_at = ring_rows(way, step)
@@ -166,7 +229,7 @@
             src_ref=part.at[ring_rows_of(way, step, piece)],
             dst_ref=ring_in.at[way, step, pl.ds(piece * (half // CUTS), half // CUTS)],
             send_sem=r_send.at[way, step, piece], recv_sem=r_recv.at[way, step, piece],
-            device_id={"cell": cell_of(x, z + 1 - 2 * way)}, device_id_type=MESH,
+            device_id={"cell": cell_of(x, z + 1 - 2 * way + nz)}, device_id_type=MESH,
         )
 
     def take(way, step, target, piece):
@@ -174,13 +237,17 @@
         at = ring_rows_of(target[0], target[1], piece)
         part[at, :] = part[at, :] + ring_in[way, step, pl.ds(piece * (half // CUTS), half // CUTS)]
 
-    def ring_step(step, kernels):
-        acc = jnp.zeros((chunk, width), jnp.float32)
+    def ring_step(steps, kernels):
+        acc = jnp.zeros((len(steps) * chunk, width), jnp.float32)
         for j in range(0, cells, WIDE):
             acc += times_members(kernels(j), j)
-        part[ring_rows(0, step), :] = acc[:half]
-        part[ring_rows(1, step), :] = acc[half:]
-
+        for n, step in enumerate(steps):
+            part[ring_rows(0, step), :] = acc[n * chunk:n * chunk + half]
+            part[ring_rows(1, step), :] = acc[n * chunk + half:(n + 1) * chunk]
+        for step in steps:
+            ring_event(step)
+
+    def ring_event(step):
         for piece in range(CUTS):
             for way in range(2):
                 @pl.when(step > 1)
@@ -190,21 +257,40 @@
                 if way == 0:
                     ring_copy(0, step, piece).start()
                 else:
-                    @pl.when(step < nz - 2)
-                    def _():
-                        ring_copy(1, step, piece).start()
+                    ring_copy(1, step, piece).start()
 
     def built_step(step, carry):
-        ring_step(step, lambda j: ahead[step, :, j:j + WIDE])
+        ring_step([step], lambda j: ahead[step, :, j:j + WIDE])
         return carry
 
-    def fresh_step(step, carry):
-        place = places(step)
-        ring_step(step, lambda j: kernel_of(place, j))
+    def fresh_step(i, carry):
+        steps = [AHEAD[-1] + PAIR * i + n for n in range(PAIR)]
+        place = [jnp.concatenate(rows, axis=0) for rows in zip(*(places(step) for step in steps))]
+        ring_step(steps, lambda j: kernel_of(place, j))
         return carry
 
     lax.fori_loop(0, AHEAD[-1], built_step, 0)
-    lax.fori_loop(AHEAD[-1], nz, fresh_step, 0)
+    lax.fori_loop(0, (nz - 2 - AHEAD[-1]) // PAIR, fresh_step, 0)
+
+    def last_step(way, carry):
+        ats = [ring_rows(way, nz - 2), ring_rows(way, nz - 1)]
+        place = places_at(ats)
+        acc = jnp.zeros((chunk, width), jnp.float32)
+        for j in range(0, cells, WIDE):
+            acc += times_members(kernel_of(place, j), j)
+        part[ats[0], :] = acc[:half]
+        part[ats[1], :] = acc[half:]
+        for piece in range(CUTS):
+            for step in (nz - 2, nz - 1):
+                take(way, step - 2, (way, step), piece)
+
+                @pl.when(way == 0)
+                def _():
+                    ring_copy(0, step, piece).start()
+
+        return carry
+
+    lax.fori_loop(0, 2, last_step, 0)
     for step in (nz - 2, nz - 1):
         for piece in range(CUTS):
             take(0, step, (1, step), piece)
@@ -291,7 +377,6 @@
     for j in range(0, cells, WIDE):
         exact = full[:, j:j + WIDE]
         rest[:, j:j + WIDE] = (exact - low[:, j:j + WIDE].astype(jnp.float32)).astype(jnp.bfloat16)
-    saves[1].start()
     over_plane(lambda o: scatter(o).wait_recv())
     eighth[...] = rows[spot(here), :] + jnp.sum(plane_in[...], axis=0)
     over_z(lambda o: along(o).start())
@@ -314,101 +399,19 @@
     total[spot(here), :] = eighth[...] + jnp.sum(z_in[...], axis=0)
     over_plane(lambda o: gather(o).start())
     over_z(lambda o: along(o).wait_send())
-    for c in saves:
-        c.wait()
     over_plane(lambda o: arrived(o).wait_recv())
-    gram_out[...] = total[0:width, :]
-    cross_out[...] = total[pl.ds(pl.multiple_of(width + obs * mine, mine), mine), :]
-    over_plane(lambda o: gather(o).wait_send())
-
-
-def pair_inverse(a, b, d):
-    scale = 1.0 / (a * d - b * b)
-    return d * scale, -b * scale, a * scale
-
-
-def quad_inverse(d):
-    p0, p1, p2 = pair_inverse(d[0][0], d[1][0], d[1][1])
-    q = [[d[2][0], d[3][0]], [d[2][1], d[3][1]]]
-    u = [[p0 * q[0][j] + p1 * q[1][j] for j in range(2)], [p1 * q[0][j] + p2 * q[1][j] for j in range(2)]]
-    s = [[d[2 + i][2 + j] - (q[0][i] * u[0][j] + q[1][i] * u[1][j]) for j in range(i + 1)] for i in range(2)]
-    s0, s1, s2 = pair_inverse(s[0][0], s[1][0], s[1][1])
-    v = [[u[i][0] * s0 + u[i][1] * s1, u[i][0] * s1 + u[i][1] * s2] for i in range(2)]
-    top = [[p0 + v[0][0] * u[0][0] + v[0][1] * u[0][1]],
-           [p1 + v[1][0] * u[0][0] + v[1][1] * u[0][1], p2 + v[1][0] * u[1][0] + v[1][1] * u[1][1]]]
-    return [
-        [top[0][0], top[1][0], -v[0][0], -v[0][1]],
-        [top[1][0], top[1][1], -v[1][0], -v[1][1]],
-        [-v[0][0], -v[1][0], s0, s1],
-        [-v[0][1], -v[1][1], s1, s2],
-    ]
-
-
-def solve_kernel(gram, cross, high_in, low_in, out, high, low, sem):
-    width, cells = high.shape
-    fetches = [pltpu.make_async_copy(high_in, high, sem.at[0]), pltpu.make_async_copy(low_in, low, sem.at[1])]
-    for c in fetches:
-        c.start()
-    lane = lax.broadcasted_iota(jnp.int32, (SUB, LANES), 1)
-    row = lax.broadcasted_iota(jnp.int32, (SUB, LANES), 0)
-    tiles = [
-        gram[i:i + SUB, :] + jnp.where(row + i == lane, width - 1.0, 0.0) for i in range(0, width, SUB)
-    ]
-    tiles += [cross[i:i + SUB, :] for i in range(0, cross.shape[0], SUB)]
-    for k in range(0, width, 4):
-        live = range((k + 4) // SUB, len(tiles))
-        home, base = k // SUB, k % SUB
-        pivot = tiles[home]
-
-        def spread(tile, at):
-            return jnp.broadcast_to(tile[:, at:at + 1], (SUB, LANES))
-
-        def level(tile, at):
-            return jnp.broadcast_to(tile[at:at + 1, :], (SUB, LANES))
-
-        pivot_cols = [spread(pivot, k + j) for j in range(4)]
-        block = [[level(pivot_cols[j], base + i) for j in range(i + 1)] for i in range(4)]
-        inv = quad_inverse(block)
-        steps = [level(pivot, base + i) for i in range(4)]
-        moved = []
-        for i in range(4):
-            t = (inv[i][0] * steps[0] + inv[i][1] * steps[1]) + (inv[i][2] * steps[2] + inv[i][3] * steps[3])
-            for m in range(4):
-                t = jnp.where(lane == k + m, -inv[i][m], t)
-            moved.append(t)
-        for n in live:
-            cols = pivot_cols if n == home else [spread(tiles[n], k + j) for j in range(4)]
-            kept = jnp.where((lane >= k) & (lane < k + 4), 0.0, tiles[n])
-            tiles[n] = kept - ((cols[0] * moved[0] + cols[1] * moved[1]) + (cols[2] * moved[2] + cols[3] * moved[3]))
-    weights = jnp.concatenate(tiles[width // SUB:], axis=0)
+
+    mine_cross = total[pl.ds(pl.multiple_of(width + obs * mine, mine), mine), :]
+    weights = solve_rows([total[i:i + SUB, :] for i in range(0, width, SUB)], mine_cross)
     weights = weights - jnp.mean(weights, axis=1, keepdims=True)
     upper = weights.astype(jnp.bfloat16)
     lower = (weights - upper.astype(jnp.float32)).astype(jnp.bfloat16)
     both = jnp.concatenate([upper, lower], axis=0)
-    for c in fetches:
-        c.wait()
-    n = upper.shape[0]
-    for j in range(0, cells, 512):
-        main = jnp.dot(both, high[:, j:j + 512], preferred_element_type=jnp.float32)
-        rest = jnp.dot(upper, low[:, j:j + 512], preferred_element_type=jnp.float32)
-        out[:, j:j + 512] = main[:n] + (main[n:] + rest)
-
-
-def increments(gram, cross, high, low):
-    width, cells = high.shape
-    vmem = pl.BlockSpec(memory_space=pltpu.VMEM)
-    return pl.pallas_call(
-        solve_kernel,
-        out_shape=jax.ShapeDtypeStruct((cross.shape[0], cells), jnp.float32),
-        in_specs=[vmem, vmem, pl.BlockSpec(memory_space=pl.ANY), pl.BlockSpec(memory_space=pl.ANY)],
-        out_specs=vmem,
-        scratch_shapes=[
-            pltpu.VMEM((width, cells), jnp.bfloat16),
-            pltpu.VMEM((width, cells), jnp.bfloat16),
-            pltpu.SemaphoreType.DMA((2,)),
-        ],
-        compiler_params=pltpu.CompilerParams(vmem_limit_bytes=64 * 2**20),
-    )(gram, cross, high, low)
+    for j in range(0, cells, WIDE):
+        main = jnp.dot(both, low[:, j:j + WIDE], preferred_element_type=jnp.float32)
+        small = jnp.dot(upper, rest[:, j:j + WIDE], preferred_element_type=jnp.float32)
+        out[:, j:j + WIDE] = main[:mine] + (main[mine:] + small)
+    over_plane(lambda o: gather(o).wait_send())
 
 
 def per_device(nx, ny, nz, station_xy, station_alt, cell_xy, cell_depth, members, targets, noise_var):
@@ -422,18 +425,12 @@
     thin = 2 * width // (nx * no)
     f32 = jnp.float32
     vmem = pl.BlockSpec(memory_space=pltpu.VMEM)
-    anyw = pl.BlockSpec(memory_space=pl.ANY)
     dma = pltpu.SemaphoreType.DMA
-    high, low, gram, cross = pl.pallas_call(
+    increment = pl.pallas_call(
         functools.partial(sums_kernel, nx, ny, nz),
-        out_shape=(
-            jax.ShapeDtypeStruct((width, cells), jnp.bfloat16),
-            jax.ShapeDtypeStruct((width, cells), jnp.bfloat16),
-            jax.ShapeDtypeStruct((width, width), f32),
-            jax.ShapeDtypeStruct((mine, width), f32),
-        ),
+        out_shape=jax.ShapeDtypeStruct((mine, cells), f32),
         in_specs=[pl.BlockSpec(memory_space=pltpu.HBM)] * 7,
-        out_specs=(anyw, anyw, vmem, vmem),
+        out_specs=vmem,
         scratch_shapes=[
             pltpu.VMEM((2, stations), f32),
             pltpu.VMEM((1, stations), f32),
@@ -460,13 +457,13 @@
             dma((nx * no - 1,)), dma((nx * no - 1,)),
             dma((nz - 1,)), dma((nz - 1,)),
             dma((nx * no - 1,)), dma((nx * no - 1,)),
-            dma((9,)),
+            dma((7,)),
         ],
         compiler_params=pltpu.CompilerParams(
             collective_id=0, has_side_effects=True, vmem_limit_bytes=64 * 2**20
         ),
     )(station_xy, station_alt[None], cell_xy, cell_depth[None], own, targets, noise_var[None])
-    return increments(gram, cross, high, low).T
+    return increment.T
 
 
 def solution(mesh):

time: 101 us -> 97.2 us (0.962)
  Pallas kernels: 100 us -> 95.3 us
  local copies, waits for them, and re-layouts: 0 us -> 1.67 us
    pallas_call x2 -> x1, Pallas kernels: 100 us -> 95.3 us  [per_device(): pl.pallas_call(functools.partial(sums_kernel, nx, ny, nz), out_shape=jax....]
    unnamed x0 -> x1, local copies, waits for them, and re-layouts: none -> 1.67 us
where the time goes in v4:
time: 97.2 us; the launch traced here: 97 us
  Pallas kernels  95.3 us (98%)
  local copies, waits for them, and re-layouts  1.67 us (2%)
    pallas_call x1, Pallas kernels, per_device(): pl.pallas_call(functools.partial(sums_kernel, nx, ny, nz), out_shape=jax....  95.3 us

profile of v4, /device:TPU:1, one launch (start us, length us, event | category | flops | bytes accessed | tf_op | source)
XLA Modules:
  0.0 97.0 jit_solution(169825437579363004)
XLA Ops:
  0.0 95.3 %shard_map.73 = f32[16,4096]{1,0:T(8,128)} custom-call(f32[2,4096]{1,0:T(2,128)} %xy_in.1, f32[1,4096]{1,0:T(1,128)} %bitcast.7, f32[2,4096]{1,0:T(2,128)} %cell_xy_in.1, f32[1,4096]{1,0:T(1,128)} %bitcast.8, f32[16,4096]{1,0:T(8,128)} %bitcast.6, f32[4096,128]{1,0:T(8,128)} %targets.1, f32[1,4096]{1,0:T(1,128)} %bitcast.9), custom_call_target="tpu_custom_call" | custom-call | tf_op jit(solution)/shard_map/pallas_call | solution.py:429
  95.4 1.7 %copy.9 = f32[4096,16]{0,1:T(8,128)} copy(f32[4096,16]{0,1:T(8,128)} %bitcast.5) | data formatting | bytes 524288

commit v5 on v4

--- a/solution.py
+++ b/solution.py
@@ -326,7 +326,7 @@
         return pl.ds(pl.multiple_of(piece * thin, thin), thin)
 
     def other(o):
-        xx, oo = lax.rem(x + o // no, nx), lax.rem(obs + lax.rem(o, no), no)
+        xx, oo = lax.rem(x + o // no, nx), lax.rem(obs + o % no, no)
         return xx * no + oo, {"cell": xx * nz + z, "obs": oo}
 
     def scatter(o):
@@ -349,7 +349,7 @@
         )
 
     def arrived(o):
-        xx, oo = lax.rem(x + nx - o // no, nx), lax.rem(obs + no - lax.rem(o, no), no)
+        xx, oo = lax.rem(x + nx - o // no, nx), lax.rem(obs + no - o % no, no)
         at = spot(xx * no + oo)
         return pltpu.make_async_remote_copy(
             src_ref=total.at[at], dst_ref=total.at[at],
@@ -357,21 +357,23 @@
         )
 
     def fan(i, middle):
-        return middle + ((i + 1) // 2) * (1 - 2 * lax.rem(i, 2))
+        return middle + ((i + 1) // 2) * (1 - 2 * (i % 2))
 
     def over_plane(action):
         def one(i, carry):
-            action(fan(i // no, nx // 2) * no + fan(lax.rem(i, no), no // 2))
+            action(fan(i // no, nx // 2) * no + fan(i % no, no // 2))
             return carry
 
-        lax.fori_loop(0, nx * no - 1, one, 0)
+        for i in range(nx * no - 1):
+            one(i, 0)
 
     def over_z(action):
         def one(i, carry):
             action(fan(i, nz // 2))
             return carry
 
-        lax.fori_loop(0, nz - 1, one, 0)
+        for i in range(nz - 1):
+            one(i, 0)
 
     over_plane(lambda o: scatter(o).start())
     for j in range(0, cells, WIDE):

time: 97.2 us -> 95.1 us (0.978)
  Pallas kernels: 95.3 us -> 93.3 us
    pallas_call x1, Pallas kernels: 95.3 us -> 93.3 us  [per_device(): pl.pallas_call(functools.partial(sums_kernel, nx, ny, nz), out_shape=jax....]
where the time goes in v5:
time: 95.1 us; the launch traced here: 95 us
  Pallas kernels  93.3 us (98%)
  local copies, waits for them, and re-layouts  1.67 us (2%)
    pallas_call x1, Pallas kernels, per_device(): pl.pallas_call(functools.partial(sums_kernel, nx, ny, nz), out_shape=jax....  93.3 us

profile of v5, /device:TPU:1, one launch (start us, length us, event | category | flops | bytes accessed | tf_op | source)
XLA Modules:
  0.0 95.0 jit_solution(1258003742817288690)
XLA Ops:
  0.0 93.3 %shard_map.73 = f32[16,4096]{1,0:T(8,128)} custom-call(f32[2,4096]{1,0:T(2,128)} %xy_in.1, f32[1,4096]{1,0:T(1,128)} %bitcast.7, f32[2,4096]{1,0:T(2,128)} %cell_xy_in.1, f32[1,4096]{1,0:T(1,128)} %bitcast.8, f32[16,4096]{1,0:T(8,128)} %bitcast.6, f32[4096,128]{1,0:T(8,128)} %targets.1, f32[1,4096]{1,0:T(1,128)} %bitcast.9), custom_call_target="tpu_custom_call" | custom-call | tf_op jit(solution)/shard_map/pallas_call | solution.py:431
  93.3 1.7 %copy.9 = f32[4096,16]{0,1:T(8,128)} copy(f32[4096,16]{0,1:T(8,128)} %bitcast.5) | data formatting | bytes 524288
